TPU v7x, 32 devices: a whole 2x2x4 slice. The times are simulated.
32 devices in a mesh: groups: 2 (over y), seq: 4 (over z), head: 2 (over x), rep: 2 (over core).
Axes of the slice: x: 2, y: 2, z: 4, core: 2. Of those that a mesh axis runs over, the one named last changes fastest.
Arguments:
- ssd_input: bfloat16 [4096, 1024], P(('groups', 'seq', 'rep'), 'head'), parts along dimension 0, may hold values from -6 to 6
- state_in: bfloat16 [4096, 128], P(('groups', 'seq', 'rep')), parts along dimension 0, may hold values from -6 to 6
- state_out: bfloat16 [4096, 128], P(('groups', 'seq', 'rep')), parts along dimension 0, may hold values from -0.5 to 0.5
- log_keep: float32 [4096, 16], P(('groups', 'seq', 'rep'), 'head'), parts along dimension 0, may hold values from -1 to 0
- skip_gain: float32 [16], P('head'), may hold values from 0.5 to 1.5
- queries: bfloat16 [4096, 1024], P(('groups', 'seq', 'rep'), 'head'), parts along dimension 0, may hold values from -8 to 8
- key_rows: bfloat16 [4096, 1024], P(('groups', 'seq', 'rep'), 'head'), parts along dimension 0, may hold values from -8 to 8
- cover_mask: int32 [16, 8], P('groups'), parts along dimension 0, may hold values from 0 to 1, as said below
- out_grad: bfloat16 [4096, 1024], P(('groups', 'seq', 'rep'), 'head'), parts along dimension 0, may hold values from -6 to 6
Outputs:
- attended: bfloat16 [4096, 1024], P(('groups', 'seq', 'rep'), 'head'), parts along dimension 0
- grad_query: bfloat16 [4096, 1024], P(('groups', 'seq', 'rep'), 'head'), parts along dimension 0
- grad_key: bfloat16 [4096, 1024], P(('groups', 'seq', 'rep'), 'head'), parts along dimension 0
- grad_input: bfloat16 [4096, 1024], P(('groups', 'seq', 'rep'), 'head'), parts along dimension 0
There are 2 independent parts, one for each index of `groups`. A program takes and returns all parts, laid end to end along the dimension named above; an argument that names none is the same for every part. Nothing has to cross between parts.
Inputs may be any that keep to these rules, and one draw needn't show every extreme that they name: `cover_mask`: Symmetric, ones on the diagonal, zero for views more than 3 apart; at least one view is covisible with every view within 3 of it.
All inputs are finite; a program needn't handle non-finite values.
Results may differ from a plain program's by a relative error of at most 0.012.
Values may be sent and summed in bfloat16 or wider, within the bound.
A program may use at most 64 MiB of HBM per device.

v0:
```python
import math

import jax
import jax.numpy as jnp
from jax import lax
from jax.sharding import PartitionSpec as P

HD = 64
BAND = 3


highest = lax.Precision.HIGHEST


def carried_in(part, axis, combine, identity):
    place = lax.axis_index(axis)
    gathered = jax.tree.map(lambda a: lax.all_gather(a, axis), part)
    state = jax.tree.map(lambda a, e: jnp.zeros_like(a) + jnp.asarray(e, a.dtype), part, identity)

    def one(turn, state):
        return combine(
            state, jax.tree.map(lambda a: lax.dynamic_index_in_dim(a, turn, 0, False), gathered)
        )

    return lax.fori_loop(0, place, one, state)


def passed_along(value, axis, steps):
    count = lax.axis_size(axis)
    leading, last = (max(0, -steps), min(count, count - steps))
    return lax.ppermute(value, axis, [(source, source + steps) for source in range(leading, last)])


def entering_2(value, axis, combine, identity):
    peers, position = (lax.axis_size(axis), lax.axis_index(axis))
    everything = jax.tree.map(
        lambda part, kind: lax.all_gather(part.astype(kind), axis),
        value,
        (jnp.bfloat16, jnp.bfloat16),
    )
    start = jax.tree.map(
        lambda part, zero: jnp.broadcast_to(jnp.asarray(zero, part.dtype), part.shape),
        value,
        identity,
    )

    def turn(k, before):
        at = peers - 1 - k
        reached = at > position
        new = combine(
            before, jax.tree.map(lambda part, own: part[at].astype(own.dtype), everything, value)
        )
        return jax.tree.map(lambda a, b: jnp.where(reached, a, b), new, before)

    return lax.fori_loop(0, peers, turn, start)


def chain_join(earlier, later):
    return (earlier[0] * later[0], later[0][:, None, None] * earlier[1] + later[1])


def local_terms(in_rows, out_rows, keep_rows):
    rows = keep_rows.shape[0]
    cumul = jnp.cumsum(keep_rows, axis=0)
    gain = jnp.sqrt(-jnp.expm1(2.0 * keep_rows))
    lower = lax.broadcasted_iota(jnp.int32, (rows, rows), 0) >= lax.broadcasted_iota(
        jnp.int32, (rows, rows), 1
    )
    leading = cumul.T
    gaps = leading[:, :, None] - leading[:, None, :]
    decay = jnp.where(lower[None], jnp.exp(jnp.where(lower[None], gaps, 0.0)), 0.0)
    intersection = jnp.dot(out_rows, in_rows.T, precision=highest)
    mixing = decay * intersection[None] * gain.T[:, None, :]
    weight = jnp.exp(cumul[-1][None, :] - cumul) * gain
    return (cumul, mixing, weight)


def block_scores(query_heads, key_heads, scale):
    return (
        jnp.einsum("rhp,khp->hrk", query_heads, key_heads, preferred_element_type=jnp.float32)
        * scale
    )


def block_grads(query_heads, grad_heads, key_heads, value_heads, log_total, correction, scale):
    shares = jnp.exp(block_scores(query_heads, key_heads, scale) - log_total[:, :, None])
    weights = shares.astype(jnp.bfloat16)
    share_grad = jnp.einsum(
        "rhp,khp->hrk", grad_heads, value_heads, preferred_element_type=jnp.float32
    )
    slopes = (shares * (share_grad - correction[:, :, None])).astype(jnp.bfloat16)
    return (weights, slopes)


def local(
    ssd_input, state_in, state_out, log_keep, skip_gain, queries, key_rows, cover_mask, out_grad
):
    rows = queries.shape[0]
    width = queries.shape[1]
    local_heads = log_keep.shape[1]
    scale = 1.0 / math.sqrt(HD)
    inputs = ssd_input.astype(jnp.float32).reshape(rows, local_heads, HD)
    in_rows = state_in.astype(jnp.float32)
    out_rows = state_out.astype(jnp.float32)
    cumul, mixing, weight = local_terms(in_rows, out_rows, log_keep)
    total_decay = jnp.exp(cumul[-1])
    state_sum = jnp.einsum("sn,shp->hnp", in_rows, weight[:, :, None] * inputs, precision=highest)
    identity = (jnp.ones_like(total_decay), jnp.zeros_like(state_sum))
    entering = carried_in((total_decay, state_sum), ("seq", "rep"), chain_join, identity)[1]
    inner = jnp.einsum("hts,shp->thp", mixing, inputs, precision=highest)
    carried = jnp.exp(cumul)[:, :, None] * jnp.einsum(
        "tn,hnp->thp", out_rows, entering, precision=highest
    )
    values = (
        (inner + carried + skip_gain[None, :, None] * inputs)
        .reshape(rows, width)
        .astype(jnp.bfloat16)
    )
    view = lax.axis_index("seq") * lax.axis_size("rep") + lax.axis_index("rep")
    offsets = list(range(-BAND, BAND + 1))
    centre = BAND
    padded_cover = jnp.pad(cover_mask, BAND)
    row_flags = lax.dynamic_slice(padded_cover, (view + BAND, view), (1, 2 * BAND + 1))[0]
    paired = jnp.concatenate([key_rows, values], axis=1)
    blocks = []
    for offset in offsets:
        if offset == 0:
            neighbour = paired
        else:
            neighbour = passed_along(paired, ("seq", "rep"), -offset)
        blocks.append(
            (
                neighbour[:, :width].reshape(rows, local_heads, HD),
                neighbour[:, width:].reshape(rows, local_heads, HD),
            )
        )
    query_heads = queries.reshape(rows, local_heads, HD)
    grad_heads = out_grad.reshape(rows, local_heads, HD)
    own_scores = block_scores(query_heads, blocks[centre][0], scale)
    peak = jnp.max(own_scores, axis=-1)
    total = jnp.sum(jnp.exp(own_scores - peak[:, :, None]), axis=-1)
    for index in range(len(offsets)):
        if index == centre:
            continue

        def widen(carry, key_heads=blocks[index][0]):
            old_peak, old_total = carry
            scores = block_scores(query_heads, key_heads, scale)
            new_peak = jnp.maximum(old_peak, jnp.max(scores, axis=-1))
            new_total = old_total * jnp.exp(old_peak - new_peak) + jnp.sum(
                jnp.exp(scores - new_peak[:, :, None]), axis=-1
            )
            return (new_peak, new_total)

        peak, total = lax.cond(row_flags[index] > 0, widen, lambda carry: carry, (peak, total))
    log_total = peak + jnp.log(total)
    gathered = jnp.zeros((rows, local_heads, HD), jnp.float32)
    for index in range(len(offsets)):

        def collect(carry, key_heads=blocks[index][0], value_heads=blocks[index][1]):
            weights = jnp.exp(
                block_scores(query_heads, key_heads, scale) - log_total[:, :, None]
            ).astype(jnp.bfloat16)
            return carry + jnp.einsum(
                "hrk,khp->rhp", weights, value_heads, preferred_element_type=jnp.float32
            )

        gathered = lax.cond(row_flags[index] > 0, collect, lambda carry: carry, gathered)
    attended = gathered.reshape(rows, width).astype(jnp.bfloat16)
    attended_heads = lax.optimization_barrier(attended).reshape(rows, local_heads, HD)
    correction = jnp.sum(
        grad_heads.astype(jnp.float32) * attended_heads.astype(jnp.float32), axis=-1
    ).T
    query_sum = jnp.zeros((rows, local_heads, HD), jnp.float32)
    returned = jnp.zeros((rows, 2 * width), jnp.float32)
    for index, offset in enumerate(offsets):

        def backward_block(carry, key_heads=blocks[index][0], value_heads=blocks[index][1]):
            weights, slopes = block_grads(
                query_heads, grad_heads, key_heads, value_heads, log_total, correction, scale
            )
            query_part = (
                jnp.einsum("hrk,khp->rhp", slopes, key_heads, preferred_element_type=jnp.float32)
                * scale
            )
            key_part = (
                jnp.einsum("hrk,rhp->khp", slopes, query_heads, preferred_element_type=jnp.float32)
                * scale
            )
            value_part = jnp.einsum(
                "hrk,rhp->khp", weights, grad_heads, preferred_element_type=jnp.float32
            )
            joined = jnp.concatenate(
                [key_part.reshape(rows, width), value_part.reshape(rows, width)], axis=1
            )
            return (carry + query_part, joined)

        def empty_block(carry):
            return (carry, jnp.zeros((rows, 2 * width), jnp.float32))

        query_sum, partial_sum = lax.cond(
            row_flags[index] > 0, backward_block, empty_block, query_sum
        )
        if offset == 0:
            returned = returned + partial_sum
        else:
            returned = returned + passed_along(partial_sum, ("seq", "rep"), offset)
    key_grads = returned[:, :width]
    value_grads = returned[:, width:]
    grad_query = query_sum.reshape(rows, width).astype(jnp.bfloat16)
    grad_key = key_grads.astype(jnp.bfloat16)
    grad_value = lax.optimization_barrier(value_grads.astype(jnp.bfloat16))
    value_heads_grad = grad_value.astype(jnp.float32).reshape(rows, local_heads, HD)
    upstream = jnp.einsum(
        "sn,shp->hnp", out_rows, jnp.exp(cumul)[:, :, None] * value_heads_grad, precision=highest
    )
    leaving = entering_2((total_decay, upstream), ("seq", "rep"), chain_join, identity)[1]
    inner_back = jnp.einsum("hts,thp->shp", mixing, value_heads_grad, precision=highest)
    carried_back = weight[:, :, None] * jnp.einsum(
        "sn,hnp->shp", in_rows, leaving, precision=highest
    )
    grad_input = (
        (inner_back + carried_back + skip_gain[None, :, None] * value_heads_grad)
        .reshape(rows, width)
        .astype(jnp.bfloat16)
    )
    return (attended, grad_query, grad_key, grad_input)


def solution(mesh):
    return jax.shard_map(
        local,
        mesh=mesh,
        in_specs=(
            P(("groups", "seq", "rep"), "head"),
            P(("groups", "seq", "rep"), None),
            P(("groups", "seq", "rep"), None),
            P(("groups", "seq", "rep"), "head"),
            P("head"),
            P(("groups", "seq", "rep"), "head"),
            P(("groups", "seq", "rep"), "head"),
            P("groups", None),
            P(("groups", "seq", "rep"), "head"),
        ),
        out_specs=(
            P(("groups", "seq", "rep"), "head"),
            P(("groups", "seq", "rep"), "head"),
            P(("groups", "seq", "rep"), "head"),
            P(("groups", "seq", "rep"), "head"),
        ),
        check_vma=False,
    )
```

profile of v0, /device:TPU:0, one launch (start us, length us, event | category | flops | bytes accessed | tf_op | source)
XLA Modules:
  0.0 294.3 jit_solution(7325545365733592919)
XLA Ops:
  10.9 2.0 convolution_bitcast_fusion.2
  14.2 13.4 %all-gather.2 = f32[8,1,8]{2,1,0:T(1,128)S(1)} all-gather(f32[1,1,8]{2,1,0:T(1,128)S(1)} %bitcast.396), channel_id=1, replica_groups=mesh['groups'=2,'seq'=4,'head'=2,'rep'=2] {'seq','rep'}, dimensions={0}, use_global_device_ids=true | all-gather | bytes 288 | tf_op jit(solution)/shard_map/all_gather | solution.py:17
  29.7 15.1 %all-gather.7.cloned.1.call-done = f32[64,128,64]{1,2,0:T(8,128)} async-done(((f32[8,128,64]{1,2,0:T(8,128)}), f32[64,128,64]{1,2,0:T(8,128)}) %all-gather.7.cloned.1.call-update) | async-done | bytes 2097168 | tf_op jit(solution)/shard_map/all_gather | solution.py:17
  47.2 7.6 %collective-permute-start = (bf16[256,1024]{1,0:T(8,128)(2,1)}, bf16[256,1024]{1,0:T(8,128)(2,1)}, u32[]{:S(2)}, u32[]{:S(2)}) collective-permute-start(bf16[256,1024]{1,0:T(8,128)(2,1)} %pad_maximum_fusion.7), channel_id=1, source_target_pairs={{0,5},{1,8},{4,9},{5,12},{8,13},{2,7},{3,10},{6,11},{7,14},{10,15}... | collective-permute-start | bytes 1572872 | tf_op jit(solution)/shard_map/ppermute | solution.py:31
  55.4 6.4 %collective-permute-start.1 = (bf16[256,1024]{1,0:T(8,128)(2,1)}, bf16[256,1024]{1,0:T(8,128)(2,1)}, u32[]{:S(2)}, u32[]{:S(2)}) collective-permute-start(bf16[256,1024]{1,0:T(8,128)(2,1)} %pad_maximum_fusion.7), channel_id=1, source_target_pairs={{0,4},{1,5},{4,8},{5,9},{8,12},{9,13},{2,6},{3,7},{6,10},{7,11},{1... | collective-permute-start | bytes 1572872 | tf_op jit(solution)/shard_map/ppermute | solution.py:31
  62.2 2.5 collective-permute-start.2
  80.5 17.2 %collective-permute-done.4 = bf16[256,1024]{1,0:T(8,128)(2,1)} collective-permute-done((bf16[256,1024]{1,0:T(8,128)(2,1)}, bf16[256,1024]{1,0:T(8,128)(2,1)}, u32[]{:S(2)}, u32[]{:S(2)}) %collective-permute-start.4) | collective-permute-done | bytes 524320 | tf_op jit(solution)/shard_map/ppermute | solution.py:31
  106.5 1.9 copy.120
  110.1 1.8 conditional.30
  112.0 1.8 copy.122
  113.8 1.8 conditional.31
  113.8 1.8 fusion.31
  116.5 1.8 conditional.32
  121.7 4.7 %conditional.36 = (f32[256,8,64]{0,2,1:T(8,128)S(1)}, f32[256,1024]{1,0:T(8,128)}) conditional(s32[]{:T(128)} %bitcast.47, f32[256,8,64]{0,2,1:T(8,128)S(1)} %get-tuple-element.612, (bf16[256,8,64]{0,2,1:T(8,128)(2,1)S(1)}, bf16[256,8,64]{0,2,1:T(8,128)(2,1)S(1)}, f32[8,256]{1,0:T(8,128)S(1)}, bf16[256,8,64]{0,2,1:T(8,128)(2,1)S(1)}, ...), branch_computations={%region_51.52_spmd, %region_52.53_spmd} | conditional | flops 340393984 | bytes 17588240 | solution.py:201
  126.4 4.1 %conditional.37 = (f32[256,8,64]{0,2,1:T(8,128)S(1)}, f32[256,1024]{0,1:T(8,128)S(1)}) conditional(s32[]{:T(128)} %bitcast.46, f32[256,8,64]{0,2,1:T(8,128)S(1)} %get-tuple-element.613, (bf16[256,8,64]{0,2,1:T(8,128)(2,1)S(1)}, bf16[256,8,64]{0,2,1:T(8,128)(2,1)S(1)}, f32[8,256]{1,0:T(8,128)S(1)}, bf16[256,8,64]{0,2,1:T(8,128)(2,1)S(1)}, ...), branch_computations={%region_53.54_spmd, %region_54.55_spmd} | conditional | flops 340393984 | bytes 15491088 | solution.py:201
  126.9 2.0 multiply_convert_fusion.4
  130.5 4.2 %conditional.38 = (f32[256,8,64]{0,2,1:T(8,128)S(1)}, f32[256,1024]{0,1:T(8,128)S(1)}) conditional(s32[]{:T(128)} %bitcast.45, f32[256,8,64]{0,2,1:T(8,128)S(1)} %get-tuple-element.614, (bf16[256,8,64]{0,2,1:T(8,128)(2,1)S(1)}, bf16[256,8,64]{0,2,1:T(8,128)(2,1)S(1)}, f32[8,256]{1,0:T(8,128)S(1)}, bf16[256,8,64]{0,2,1:T(8,128)(2,1)S(1)}, ...), branch_computations={%region_55.56_spmd, %region_56.57_spmd} | conditional | flops 340393984 | bytes 15491088 | solution.py:201
  131.0 2.0 multiply_convert_fusion.5
  135.7 5.1 %conditional.39 = (f32[256,8,64]{0,2,1:T(8,128)S(1)}, f32[256,1024]{0,1:T(8,128)}) conditional(s32[]{:T(128)} %bitcast.44, f32[256,8,64]{0,2,1:T(8,128)S(1)} %get-tuple-element.615, (bf16[256,8,64]{0,2,1:T(8,128)(2,1)S(1)}, bf16[256,8,64]{0,2,1:T(8,128)(2,1)S(1)}, f32[8,256]{1,0:T(8,128)S(1)}, bf16[256,8,64]{0,2,1:T(8,128)(2,1)S(1)}, ...), branch_computations={%region_57.58_spmd, %region_58.59_spmd} | conditional | flops 340393984 | bytes 15491088 | solution.py:201
  136.2 2.0 multiply_convert_fusion.6
  140.8 2.6 copy.131
  143.4 2.3 collective-permute-start.11
  147.1 9.3 %collective-permute-start.10 = (f32[256,1024]{1,0:T(8,128)}, f32[256,1024]{1,0:T(8,128)}, u32[]{:S(2)}, u32[]{:S(2)}) collective-permute-start(f32[256,1024]{1,0:T(8,128)} %copy.130), channel_id=1, source_target_pairs={{0,4},{1,5},{4,8},{5,9},{8,12},{9,13},{2,6},{3,7},{6,10},{7,11},{1... | collective-permute-start | bytes 3145736 | tf_op jit(solution)/shard_map/ppermute | solution.py:31
  157.7 6.3 %collective-permute-start.9 = (f32[256,1024]{1,0:T(8,128)}, f32[256,1024]{1,0:T(8,128)}, u32[]{:S(2)}, u32[]{:S(2)}) collective-permute-start(f32[256,1024]{1,0:T(8,128)} %copy.129), channel_id=1, source_target_pairs={{0,1},{1,4},{4,5},{5,8},{8,9},{9,12},{12,13},{2,3},{3,6},{6,7},{7,... | collective-permute-start | bytes 3145736 | tf_op jit(solution)/shard_map/ppermute | solution.py:31
  164.0 2.6 copy.127
  173.2 8.0 %collective-permute-done.10 = f32[256,1024]{1,0:T(8,128)} collective-permute-done((f32[256,1024]{1,0:T(8,128)}, f32[256,1024]{1,0:T(8,128)}, u32[]{:S(2)}, u32[]{:S(2)}) %collective-permute-start.10) | collective-permute-done | bytes 1048608 | tf_op jit(solution)/shard_map/ppermute | solution.py:31
  181.2 15.6 %collective-permute-done.6 = f32[256,1024]{1,0:T(8,128)S(1)} collective-permute-done((f32[256,1024]{1,0:T(8,128)}, f32[256,1024]{1,0:T(8,128)S(1)}, u32[]{:S(2)}, u32[]{:S(2)}) %collective-permute-start.6) | collective-permute-done | bytes 1048608 | tf_op jit(solution)/shard_map/ppermute | solution.py:31
  196.9 26.8 %collective-permute-done.7 = f32[256,1024]{1,0:T(8,128)S(1)} collective-permute-done((f32[256,1024]{1,0:T(8,128)}, f32[256,1024]{1,0:T(8,128)S(1)}, u32[]{:S(2)}, u32[]{:S(2)}) %collective-permute-start.7) | collective-permute-done | bytes 1048608 | tf_op jit(solution)/shard_map/ppermute | solution.py:31
  223.6 3.2 %add_convert_fusion = bf16[256,1024]{1,0:T(8,128)(2,1)S(1)} fusion(f32[256,1024]{1,0:T(8,128)} %collective-permute-done.11, f32[256,1024]{1,0:T(8,128)} %collective-permute-done.10, f32[256,1024]{1,0:T(8,128)} %collective-permute-done.9, f32[256,1024]{1,0:T(8,128)} %get-tuple-element.758, f32[256,1024]{1,0:T(8,128)} %collective-permute-done.8, ...), kind=kLoop, calls=%fused_computation.176 | loop fusion | flops 1835008 | bytes 7864320 | tf_op jit(solution)/shard_map/convert.13
  229.0 22.5 %all-gather.3 = bf16[8,1,8]{2,1,0:T(2,128)(2,1)S(1)} all-gather(bf16[1,1,8]{2,1,0:T(2,128)(2,1)S(1)} %bitcast.397), channel_id=1, replica_groups=mesh['groups'=2,'seq'=4,'head'=2,'rep'=2] {'seq','rep'}, dimensions={0}, use_global_device_ids=true | all-gather | bytes 144 | tf_op jit(solution)/shard_map/all_gather | solution.py:37
  254.8 20.5 %all-gather.9.cloned.1.call-done = bf16[64,128,64]{1,2,0:T(8,128)(2,1)} async-done(((bf16[8,128,64]{1,2,0:T(8,128)(2,1)}), bf16[64,128,64]{1,2,0:T(8,128)(2,1)}) %all-gather.9.cloned.1.call-update) | async-done | bytes 1048592 | tf_op jit(solution)/shard_map/all_gather | solution.py:37
  275.3 10.4 %while.29 = (s32[]{:T(128)}, f32[8,128,64]{2,1,0:T(8,128)S(1)}, s32[]{:T(128)}, bf16[8,8]{1,0:T(8,128)(2,1)S(1)}, bf16[8,8,128,64]{2,3,1,0:T(8,128)(2,1)}, /*index=5*/s32[]{:T(128)}, s32[]{:T(128)}, s32[]{:T(128)}, s32[]{:T(128)}) while((s32[]{:T(128)}, f32[8,128,64]{2,1,0:T(8,128)S(1)}, s32[]{:T(128)}, ...), condition=%wide.region_60.61_spmd.clone, body=%wide.region_59.60_spmd.clone.sunk | while | flops 327696 | bytes 1179903 | solution.py:55
  (227 shorter events, 82.4 us)
Async XLA Ops:
  7.2 20.5 %copy-start = (bf16[256,128]{1,0:T(8,128)(2,1)S(1)}, bf16[256,128]{1,0:T(8,128)(2,1)}, u32[]{:S(2)}) copy-start(bf16[256,128]{1,0:T(8,128)(2,1)} %param.55) | copy-start | bytes 196612
  7.2 20.5 %copy-start.13 = (bf16[256,128]{1,0:T(8,128)(2,1)S(1)}, bf16[256,128]{1,0:T(8,128)(2,1)}, u32[]{:S(2)}) copy-start(bf16[256,128]{1,0:T(8,128)(2,1)} %param.54) | copy-start | bytes 196612
  7.2 6.8 %copy-start.10 = (bf16[256,512]{1,0:T(8,128)(2,1)S(1)}, bf16[256,512]{1,0:T(8,128)(2,1)}, u32[]{:S(2)}) copy-start(bf16[256,512]{1,0:T(8,128)(2,1)} %param.59) | copy-start | bytes 786436
  7.2 37.6 %all-gather.7.cloned.1.call-start = ((), (), s32[]{:S(2)}) async-start(), calls=%async_computation | async-start | bytes 2359296 | tf_op jit(solution)/shard_map/all_gather | solution.py:17
  9.9 17.7 %copy-start.21 = (f32[256,8]{0,1:T(8,128)}, f32[256,8]{0,1:T(8,128)S(1)}, u32[]{:S(2)}) copy-start(f32[256,8]{0,1:T(8,128)S(1)} %get-tuple-element.782) | copy-start | bytes 24580
  9.9 35.0 %copy-start.17 = (f32[256,8]{0,1:T(8,128)}, f32[256,8]{0,1:T(8,128)S(1)}, u32[]{:S(2)}) copy-start(f32[256,8]{0,1:T(8,128)S(1)} %get-tuple-element.781) | copy-start | bytes 24580
  10.9 16.7 %copy-start.19 = (f32[256,8]{0,1:T(8,128)}, f32[256,8]{0,1:T(8,128)S(1)}, u32[]{:S(2)}) copy-start(f32[256,8]{0,1:T(8,128)S(1)} %get-tuple-element.809) | copy-start | bytes 24580
  10.9 18.8 %copy-start.27 = (f32[8,256]{1,0:T(8,128)}, f32[8,256]{1,0:T(8,128)S(1)}, u32[]{:S(2)}) copy-start(f32[8,256]{1,0:T(8,128)S(1)} %get-tuple-element.810) | copy-start | bytes 24580
  12.9 262.4 %all-gather.9.cloned.1.call-start = ((), (), s32[]{:S(2)}) async-start(), calls=%async_computation.1 | async-start | bytes 1179648 | tf_op jit(solution)/shard_map/all_gather | solution.py:37
  46.2 9.1 %copy-start.29 = (s32[8,8]{1,0:T(8,128)S(1)}, s32[8,8]{1,0:T(8,128)}, u32[]{:S(2)}) copy-start(s32[8,8]{1,0:T(8,128)} %param.60) | copy-start | bytes 772
  47.2 25.4 %collective-permute-start = (bf16[256,1024]{1,0:T(8,128)(2,1)}, bf16[256,1024]{1,0:T(8,128)(2,1)}, u32[]{:S(2)}, u32[]{:S(2)}) collective-permute-start(bf16[256,1024]{1,0:T(8,128)(2,1)} %pad_maximum_fusion.7), channel_id=1, source_target_pairs={{0,5},{1,8},{4,9},{5,12},{8,13},{2,7},{3,10},{6,11},{7,14},{10,15}... | collective-permute-start | bytes 1572872 | tf_op jit(solution)/shard_map/ppermute | solution.py:31
  54.8 15.1 %copy-start.16 = (bf16[256,512]{1,0:T(8,128)(2,1)S(1)}, bf16[256,512]{1,0:T(8,128)(2,1)}, u32[]{:S(2)}) copy-start(bf16[256,512]{1,0:T(8,128)(2,1)} %param.61) | copy-start | bytes 786436
  55.4 21.0 %collective-permute-start.1 = (bf16[256,1024]{1,0:T(8,128)(2,1)}, bf16[256,1024]{1,0:T(8,128)(2,1)}, u32[]{:S(2)}, u32[]{:S(2)}) collective-permute-start(bf16[256,1024]{1,0:T(8,128)(2,1)} %pad_maximum_fusion.7), channel_id=1, source_target_pairs={{0,4},{1,5},{4,8},{5,9},{8,12},{9,13},{2,6},{3,7},{6,10},{7,11},{1... | collective-permute-start | bytes 1572872 | tf_op jit(solution)/shard_map/ppermute | solution.py:31
  62.2 15.3 %collective-permute-start.2 = (bf16[256,1024]{1,0:T(8,128)(2,1)}, bf16[256,1024]{1,0:T(8,128)(2,1)S(1)}, u32[]{:S(2)}, u32[]{:S(2)}) collective-permute-start(bf16[256,1024]{1,0:T(8,128)(2,1)} %pad_maximum_fusion.7), channel_id=1, source_target_pairs={{0,1},{1,4},{4,5},{5,8},{8,9},{9,12},{12,13},{2,3},{3,6},{6,7},{7,... | collective-permute-start | bytes 1572872 | tf_op jit(solution)/shard_map/ppermute | solution.py:31
  70.0 8.6 %collective-permute-start.3 = (bf16[256,1024]{1,0:T(8,128)(2,1)}, bf16[256,1024]{1,0:T(8,128)(2,1)}, u32[]{:S(2)}, u32[]{:S(2)}) collective-permute-start(bf16[256,1024]{1,0:T(8,128)(2,1)} %pad_maximum_fusion.7), channel_id=1, source_target_pairs={{1,0},{4,1},{5,4},{8,5},{9,8},{12,9},{13,12},{3,2},{6,3},{7,6},{10... | collective-permute-start | bytes 1572872 | tf_op jit(solution)/shard_map/ppermute | solution.py:31
  71.3 26.4 %collective-permute-start.4 = (bf16[256,1024]{1,0:T(8,128)(2,1)}, bf16[256,1024]{1,0:T(8,128)(2,1)}, u32[]{:S(2)}, u32[]{:S(2)}) collective-permute-start(bf16[256,1024]{1,0:T(8,128)(2,1)} %pad_maximum_fusion.7), channel_id=1, source_target_pairs={{4,0},{5,1},{8,4},{9,5},{12,8},{13,9},{6,2},{7,3},{10,6},{11,7},{1... | collective-permute-start | bytes 1572872 | tf_op jit(solution)/shard_map/ppermute | solution.py:31
  72.6 27.0 %collective-permute-start.5 = (bf16[256,1024]{1,0:T(8,128)(2,1)}, bf16[256,1024]{1,0:T(8,128)(2,1)}, u32[]{:S(2)}, u32[]{:S(2)}) collective-permute-start(bf16[256,1024]{1,0:T(8,128)(2,1)} %pad_maximum_fusion.7), channel_id=1, source_target_pairs={{5,0},{8,1},{9,4},{12,5},{13,8},{7,2},{10,3},{11,6},{14,7},{15,10}... | collective-permute-start | bytes 1572872 | tf_op jit(solution)/shard_map/ppermute | solution.py:31
  140.8 4.9 %copy-start.7 = (f32[256,1024]{0,1:T(8,128)S(1)}, f32[256,1024]{0,1:T(8,128)}, u32[]{:S(2)}) copy-start(f32[256,1024]{0,1:T(8,128)} %copy-done.6) | copy-start | bytes 3145732
  143.4 28.5 %collective-permute-start.11 = (f32[256,1024]{1,0:T(8,128)}, f32[256,1024]{1,0:T(8,128)}, u32[]{:S(2)}, u32[]{:S(2)}) collective-permute-start(f32[256,1024]{1,0:T(8,128)} %copy.131), channel_id=1, source_target_pairs={{0,5},{1,8},{4,9},{5,12},{8,13},{2,7},{3,10},{6,11},{7,14},{10,15}... | collective-permute-start | bytes 3145736 | tf_op jit(solution)/shard_map/ppermute | solution.py:31
  147.1 34.1 %collective-permute-start.10 = (f32[256,1024]{1,0:T(8,128)}, f32[256,1024]{1,0:T(8,128)}, u32[]{:S(2)}, u32[]{:S(2)}) collective-permute-start(f32[256,1024]{1,0:T(8,128)} %copy.130), channel_id=1, source_target_pairs={{0,4},{1,5},{4,8},{5,9},{8,12},{9,13},{2,6},{3,7},{6,10},{7,11},{1... | collective-permute-start | bytes 3145736 | tf_op jit(solution)/shard_map/ppermute | solution.py:31
  156.4 11.5 %copy-start.2 = (f32[256,1024]{0,1:T(8,128)S(1)}, f32[256,1024]{0,1:T(8,128)}, u32[]{:S(2)}) copy-start(f32[256,1024]{0,1:T(8,128)} %copy-done.1) | copy-start | bytes 3145732
  157.7 23.5 %collective-permute-start.9 = (f32[256,1024]{1,0:T(8,128)}, f32[256,1024]{1,0:T(8,128)}, u32[]{:S(2)}, u32[]{:S(2)}) collective-permute-start(f32[256,1024]{1,0:T(8,128)} %copy.129), channel_id=1, source_target_pairs={{0,1},{1,4},{4,5},{5,8},{8,9},{9,12},{12,13},{2,3},{3,6},{6,7},{7,... | collective-permute-start | bytes 3145736 | tf_op jit(solution)/shard_map/ppermute | solution.py:31
  164.0 6.6 %copy-start.4 = (f32[256,1024]{0,1:T(8,128)S(1)}, f32[256,1024]{0,1:T(8,128)}, u32[]{:S(2)}) copy-start(f32[256,1024]{0,1:T(8,128)} %copy-done.3) | copy-start | bytes 3145732
  166.6 14.6 %collective-permute-start.8 = (f32[256,1024]{1,0:T(8,128)}, f32[256,1024]{1,0:T(8,128)}, u32[]{:S(2)}, u32[]{:S(2)}) collective-permute-start(f32[256,1024]{1,0:T(8,128)} %copy.127), channel_id=1, source_target_pairs={{1,0},{4,1},{5,4},{8,5},{9,8},{12,9},{13,12},{3,2},{6,3},{7,6},{10... | collective-permute-start | bytes 3145736 | tf_op jit(solution)/shard_map/ppermute | solution.py:31
  169.3 27.6 %collective-permute-start.6 = (f32[256,1024]{1,0:T(8,128)}, f32[256,1024]{1,0:T(8,128)S(1)}, u32[]{:S(2)}, u32[]{:S(2)}) collective-permute-start(f32[256,1024]{1,0:T(8,128)} %copy.125), channel_id=1, source_target_pairs={{5,0},{8,1},{9,4},{12,5},{13,8},{7,2},{10,3},{11,6},{14,7},{15,10}... | collective-permute-start | bytes 3145736 | tf_op jit(solution)/shard_map/ppermute | solution.py:31
  171.9 51.7 %collective-permute-start.7 = (f32[256,1024]{1,0:T(8,128)}, f32[256,1024]{1,0:T(8,128)S(1)}, u32[]{:S(2)}, u32[]{:S(2)}) collective-permute-start(f32[256,1024]{1,0:T(8,128)} %copy.126), channel_id=1, source_target_pairs={{4,0},{5,1},{8,4},{9,5},{12,8},{13,9},{6,2},{7,3},{10,6},{11,7},{1... | collective-permute-start | bytes 3145736 | tf_op jit(solution)/shard_map/ppermute | solution.py:31
  226.8 26.4 %copy-start.15 = (f32[256,256]{1,0:T(8,128)S(1)}, f32[256,256]{1,0:T(8,128)}, u32[]{:S(2)}) copy-start(f32[256,256]{1,0:T(8,128)} %copy-done.14) | copy-start | bytes 786436
  226.8 26.4 %copy-start.24 = (pred[256,256]{1,0:T(8,128)(4,1)S(1)}, pred[256,256]{1,0:T(8,128)(4,1)}, u32[]{:S(2)}) copy-start(pred[256,256]{1,0:T(8,128)(4,1)} %copy-done.23) | copy-start | bytes 196612
  226.9 26.4 %copy-start.26 = (f32[8,256]{1,0:T(8,128)S(1)}, f32[8,256]{1,0:T(8,128)}, u32[]{:S(2)}) copy-start(f32[8,256]{1,0:T(8,128)} %copy-done.25) | copy-start | bytes 24580
  226.9 26.4 %copy-start.28 = (f32[8,256]{1,0:T(8,128)S(1)}, f32[8,256]{1,0:T(8,128)}, u32[]{:S(2)}) copy-start(f32[8,256]{1,0:T(8,128)} %copy-done.27) | copy-start | bytes 24580
  275.3 10.4 %copy-start.20 = (f32[256,8]{0,1:T(8,128)S(1)}, f32[256,8]{0,1:T(8,128)}, u32[]{:S(2)}) copy-start(f32[256,8]{0,1:T(8,128)} %copy-done.19) | copy-start | bytes 24580
  275.3 10.4 %copy-start.31 = (f32[8]{0:T(128)S(1)}, f32[8]{0:T(128)}, u32[]{:S(2)}) copy-start(f32[8]{0:T(128)} %param.57) | copy-start | bytes 100
  (12 other events, 22.3 us)
Sparse Core Ops, SparseCore 0:
  13.0 31.7 all-gather.6
  229.0 46.2 all-gather.8
where the time goes:
time: 298 us; the launch traced here: 294 us
  waiting for transfers between devices  105 us (35%)
  local copies, waits for them, and re-layouts  48.9 us (16%)
  starting transfers between devices  42.2 us (14%)
  blocking collectives  35.9 us (12%)
  matrix products  31.2 us (10%)
  between operations  19.5 us (7%)
  other arithmetic  10.6 us (4%)
    ppermute x12, waiting for transfers between devices, passed_along(): lax.ppermute(value, axis, [(source, source + steps) for source in range(l...  69 us
    ppermute x12, starting transfers between devices, passed_along(): lax.ppermute(value, axis, [(source, source + steps) for source in range(l...  42.1 us
    all_gather x1, blocking collectives, entering_2(): lax.all_gather(part.astype(kind), axis)  22.5 us
    all_gather x1, waiting for transfers between devices, entering_2(): lax.all_gather(part.astype(kind), axis)  20.5 us
    slice x12, local copies, waits for them, and re-layouts, local(): neighbour[:, width:].reshape(rows, local_heads, HD)  15.3 us
    all_gather x1, waiting for transfers between devices, carried_in(): gathered = jax.tree.map(lambda a: lax.all_gather(a, axis), part)  15.1 us
    all_gather x1, blocking collectives, carried_in(): gathered = jax.tree.map(lambda a: lax.all_gather(a, axis), part)  13.4 us
    cond x7, local copies, waits for them, and re-layouts, local(): lax.cond(row_flags[index] > 0, backward_block, empty_block, query_sum)  11.9 us
  transfers between devices with their start and end apart: 14, of which 7 were waited for; matrix products, arithmetic and copies ran while one was open for 8% of the time, Pallas kernels for 0%

commit v1 on v0

v1 whole, which is shorter than its diff:
```python
import functools

import jax
import jax.numpy as jnp
from jax import lax
from jax.experimental import pallas as pl
from jax.experimental.pallas import tpu as pltpu
from jax.sharding import PartitionSpec as P

HD = 64
BAND = 3
PAIR = 2 * HD
F32 = jnp.float32
BF16 = jnp.bfloat16
HIGHEST = lax.Precision.HIGHEST
NEIGH = [o for o in range(-BAND, BAND + 1)]


def dot(a, b, dims):
    return lax.dot_general(a, b, (dims, ((), ())), preferred_element_type=F32)


NN = ((1,), (0,))
NT = ((1,), (1,))
TN = ((0,), (0,))


def first_lanes(shape):
    return lax.broadcasted_iota(jnp.int32, shape, 1) < HD


def widened(col, p):
    rows = col.shape[0]
    return jnp.where(
        first_lanes((rows, PAIR)),
        jnp.broadcast_to(col[:, 2 * p : 2 * p + 1], (rows, PAIR)),
        jnp.broadcast_to(col[:, 2 * p + 1 : 2 * p + 2], (rows, PAIR)),
    )


def widened_all(col):
    return jnp.concatenate([widened(col, p) for p in range(col.shape[1] // 2)], axis=1)


def stacked(a):
    first = first_lanes(a.shape)
    zero = jnp.zeros_like(a)
    return jnp.concatenate([jnp.where(first, a, zero), jnp.where(first, zero, a)], axis=0)


def picked(a):
    rows = a.shape[0] // 2
    return jnp.where(first_lanes((rows, PAIR)), a[:rows], a[rows:])


def running(keep):
    rows = keep.shape[0]
    below = (
        lax.broadcasted_iota(jnp.int32, (rows, rows), 0)
        >= lax.broadcasted_iota(jnp.int32, (rows, rows), 1)
    ).astype(F32)
    cumul = lax.dot_general(below, keep, (NN, ((), ())), precision=HIGHEST, preferred_element_type=F32)
    gain = jnp.sqrt(-one_less(2.0 * keep))
    return cumul, gain


def one_less(y):
    return jnp.tanh(0.5 * y) * (jnp.exp(y) + 1.0)


def scan_terms(x_ref, b_ref, c_ref, lk_ref, skip_ref, mix_ref, local_ref, ecum_ref, wide_ref, state_ref):
    keep = lk_ref[...]
    rows, heads = keep.shape
    cumul, gain = running(keep)
    both = jnp.transpose(jnp.concatenate([cumul, gain], axis=1))
    last = cumul[rows - 1 : rows, :]
    weight = jnp.exp(last - cumul) * gain
    b = b_ref[...]
    c = c_ref[...]
    cross = dot(c, b, NT)
    lower = lax.broadcasted_iota(jnp.int32, (rows, rows), 0) >= lax.broadcasted_iota(
        jnp.int32, (rows, rows), 1
    )
    masked = jnp.where(lower, cross, 0.0)
    ecum_ref[...] = widened_all(jnp.exp(cumul))
    wide = widened_all(weight)
    wide_ref[...] = wide
    x = x_ref[...]
    state = dot(b, (wide * x.astype(F32)).astype(BF16), TN)
    nstate = state.shape[0]
    state_ref[0:nstate, :] = state.astype(BF16)
    total = jnp.broadcast_to(widened_all(jnp.exp(last)), (8, x.shape[1]))
    high = total.astype(BF16)
    low = (total - high.astype(F32)).astype(BF16)
    state_ref[nstate : nstate + 16, :] = jnp.concatenate([high, low], axis=0)
    for p in range(heads // 2):
        mixes = []
        for h in (2 * p, 2 * p + 1):
            gaps = jnp.minimum(cumul[:, h : h + 1] - both[h : h + 1, :], 0.0)
            mix = (jnp.exp(gaps) * masked * both[heads + h : heads + h + 1, :]).astype(BF16)
            mix_ref[h * rows : (h + 1) * rows, :] = mix
            mixes.append(mix)
        xp = x[:, p * PAIR : (p + 1) * PAIR]
        inner = dot(jnp.concatenate(mixes, axis=1), stacked(xp), NN)
        local_ref[:, p * PAIR : (p + 1) * PAIR] = inner + widened(skip_ref[...], p) * xp.astype(F32)


def position():
    return lax.axis_index("seq") * lax.axis_size("rep") + lax.axis_index("rep")


def decays(part, nstate):
    return part[nstate : nstate + 1, :].astype(F32) + part[nstate + 8 : nstate + 9, :].astype(F32)


def values_body(gathered_ref, c_ref, local_ref, ecum_ref, values_ref):
    nstate = c_ref.shape[1]
    me = position()
    entering = jnp.zeros((nstate, values_ref.shape[1]), F32)
    for u in range(gathered_ref.shape[0]):
        part = gathered_ref[u]
        new = decays(part, nstate) * entering + part[:nstate].astype(F32)
        entering = jnp.where(u < me, new, entering)
    carried = ecum_ref[...] * dot(c_ref[...], entering.astype(BF16), NN)
    values_ref[...] = (local_ref[...] + carried).astype(BF16)


def attention_body(flags_ref, q_ref, do_ref, k_refs, v_refs, att_ref, dq_ref, dk_ref, dv_ref, s_ref):
    count = len(k_refs)
    rows, width = q_ref.shape
    biases = [jnp.where(flags_ref[0, j] > 0, 0.0, -1e30).astype(F32) for j in range(count)]

    def one(p, _):
        lanes = pl.ds(pl.multiple_of(p * PAIR, PAIR), PAIR)
        q2 = stacked(q_ref[:, lanes] * jnp.asarray(0.125, BF16))
        do = do_ref[:, lanes]
        do2 = stacked(do)
        peak = None
        for j in range(count):
            s = dot(q2, k_refs[j][:, lanes], NT) + biases[j]
            s_ref[j] = s
            peak = s if peak is None else jnp.maximum(peak, s)
        peak = jnp.max(peak, axis=1, keepdims=True)
        total = None
        for j in range(count):
            e = jnp.exp(s_ref[j] - peak)
            s_ref[j] = e
            total = e if total is None else total + e
        inv = 1.0 / jnp.sum(total, axis=1, keepdims=True)
        out = jnp.zeros((2 * rows, PAIR), F32)
        for j in range(count):
            share = s_ref[j] * inv
            s_ref[j] = share
            out += dot(share.astype(BF16), v_refs[j][:, lanes], NN)
        att = picked(out).astype(BF16)
        att_ref[:, lanes] = att
        att2 = jnp.concatenate([att, att], axis=0).astype(F32)
        corr = jnp.sum(do2.astype(F32) * att2, axis=1, keepdims=True)
        dq = jnp.zeros((2 * rows, PAIR), F32)
        for j in range(count):
            share = s_ref[j]
            dp = dot(do2, v_refs[j][:, lanes], NT)
            slope = (share * (dp - corr)).astype(BF16)
            dq += dot(slope, k_refs[j][:, lanes], NN)
            dk_ref[j, :, lanes] = dot(slope, q2, TN).astype(BF16)
            dv_ref[j, :, lanes] = dot(share.astype(BF16), do2, TN).astype(BF16)
        dq_ref[:, lanes] = (picked(dq) * 0.125).astype(BF16)
        return 0

    lax.fori_loop(0, width // PAIR, one, 0)


def combine_body(parts, c_ref, ecum_ref, dk_ref, dv_ref, up_ref):
    dk = None
    for k_part, v_part in parts:
        k, v = k_part[...].astype(F32), v_part[...].astype(F32)
        dk, dv = (k, v) if dk is None else (dk + k, dv + v)
    dk_ref[...] = dk.astype(BF16)
    dv = dv.astype(BF16)
    dv_ref[...] = dv
    up_ref[...] = dot(c_ref[...], (ecum_ref[...] * dv.astype(F32)).astype(BF16), TN).astype(BF16)


def input_body(gathered_ref, ups_ref, b_ref, dv_ref, wide_ref, mix_ref, skip_ref, out_ref):
    nstate = b_ref.shape[1]
    rows, width = dv_ref.shape
    me = position()
    leaving = jnp.zeros((nstate, width), F32)
    for u in range(ups_ref.shape[0] - 1, -1, -1):
        new = decays(gathered_ref[u], nstate) * leaving + ups_ref[u].astype(F32)
        leaving = jnp.where(u > me, new, leaving)
    carried = wide_ref[...] * dot(b_ref[...], leaving.astype(BF16), NN)
    for p in range(width // PAIR):
        lanes = slice(p * PAIR, (p + 1) * PAIR)
        dv = dv_ref[:, lanes]
        inner = dot(mix_ref[2 * p * rows : 2 * (p + 1) * rows, :], stacked(dv), TN)
        out_ref[:, lanes] = (
            inner + carried[:, lanes] + widened(skip_ref[...], p) * dv.astype(F32)
        ).astype(BF16)


def call(body, outs, *args, scratch=(), smem=0):
    specs = [pl.BlockSpec(memory_space=pltpu.SMEM)] * smem + [
        pl.BlockSpec(memory_space=pltpu.VMEM)
    ] * (len(args) - smem)
    return pl.pallas_call(
        body,
        out_shape=[jax.ShapeDtypeStruct(s, d) for s, d in outs],
        in_specs=specs,
        out_specs=[pl.BlockSpec(memory_space=pltpu.VMEM)] * len(outs),
        scratch_shapes=list(scratch),
        compiler_params=pltpu.CompilerParams(vmem_limit_bytes=48 << 20),
    )(*args)


def passed(value, steps):
    count = lax.axis_size("seq") * lax.axis_size("rep")
    leading, last = max(0, -steps), min(count, count - steps)
    return lax.ppermute(value, ("seq", "rep"), [(i, i + steps) for i in range(leading, last)])


def local(x, b, c, lk, skip, q, k, cover, do):
    rows, width = q.shape
    heads = lk.shape[1]
    nstate = b.shape[1]
    skip = skip.reshape(1, heads)
    view = position()
    flags = lax.dynamic_slice(jnp.pad(cover, BAND), (view + BAND, view), (1, 2 * BAND + 1))
    keys = {o: (k if o == 0 else passed(k, -o)) for o in NEIGH}
    mix, base, ecum, wide, state = call(
        scan_terms,
        [((heads * rows, rows), BF16), ((rows, width), F32), ((rows, width), F32), ((rows, width), F32), ((nstate + 16, width), BF16)],
        x, b, c, lk, skip,
    )
    gathered = lax.all_gather(state, ("seq", "rep"))
    (values,) = call(values_body, [((rows, width), BF16)], gathered, c, base, ecum)
    vals = {o: (values if o == 0 else passed(values, -o)) for o in NEIGH}
    n = len(NEIGH)

    def attend(*refs):
        attention_body(refs[0], refs[1], refs[2], refs[3 : 3 + n], refs[3 + n : 3 + 2 * n], *refs[3 + 2 * n :])

    att, dq, dks, dvs = call(
        attend,
        [((rows, width), BF16), ((rows, width), BF16), ((n, rows, width), BF16), ((n, rows, width), BF16)],
        flags, q, do, *[keys[o] for o in NEIGH], *[vals[o] for o in NEIGH],
        scratch=[pltpu.VMEM((n, 2 * rows, rows), F32)], smem=1,
    )
    parts = []
    for j, o in enumerate(NEIGH):
        parts += [dks[j], dvs[j]] if o == 0 else [passed(dks[j], o), passed(dvs[j], o)]

    def combine(*refs):
        combine_body([(refs[2 * i], refs[2 * i + 1]) for i in range(n)], *refs[2 * n :])

    dk, dv, up = call(
        combine,
        [((rows, width), BF16), ((rows, width), BF16), ((nstate, width), BF16)],
        *parts, c, ecum,
    )
    ups = lax.all_gather(up, ("seq", "rep"))
    (dx,) = call(input_body, [((rows, width), BF16)], gathered, ups, b, dv, wide, mix, skip)
    return att, dq, dk, dx


def solution(mesh):
    rows = P(("groups", "seq", "rep"), "head")
    shared = P(("groups", "seq", "rep"), None)
    return jax.shard_map(
        local,
        mesh=mesh,
        in_specs=(rows, shared, shared, rows, P("head"), rows, rows, P("groups", None), rows),
        out_specs=(rows, rows, rows, rows),
        check_vma=False,
    )
```

time: 298 us -> 186 us (0.62)
  waiting for transfers between devices: 105 us -> 62.3 us
  local copies, waits for them, and re-layouts: 48.9 us -> 10.9 us
  blocking collectives: 35.9 us -> 0 us
  matrix products: 31.2 us -> 0 us
  Pallas kernels: 0 us -> 28.7 us
  starting transfers between devices: 42.2 us -> 68.8 us
  other arithmetic: 10.6 us -> 0 us
  between operations: 19.5 us -> 14.4 us
    ppermute x12 -> x24, waiting for transfers between devices: 69 us -> 25 us  [passed(): lax.ppermute(value, ('seq', 'rep'), [(i, i + steps) for i in range(leadin...]
    all_gather x2 -> x0, blocking collectives: 35.9 us -> none  [the longest x1 22.5 us: entering_2(): lax.all_gather(part.astype(kind), axis)]
    dot_general x35 -> x0, matrix products: 31.2 us -> none  [the longest x4 7.02 us: block_grads(): jnp.einsum('rhp,khp->hrk', grad_heads, value_heads, preferred_element_typ...]
    pallas_call x0 -> x5, Pallas kernels: none -> 28.7 us  [call(): pl.pallas_call(body, out_shape=[jax.ShapeDtypeStruct(s, d) for s, d in ou...]
    ppermute x12 -> x24, starting transfers between devices: 42.1 us -> 68.8 us  [passed(): lax.ppermute(value, ('seq', 'rep'), [(i, i + steps) for i in range(leadin...]
    slice x22 -> x0, local copies, waits for them, and re-layouts: 17.8 us -> none  [the longest x12 15.3 us: local(): neighbour[:, width:].reshape(rows, local_heads, HD)]
    cond x10 -> x0, local copies, waits for them, and re-layouts: 11.9 us -> none  [the longest x7 11.9 us: local(): lax.cond(row_flags[index] > 0, backward_block, empty_block, query_sum)]
    dynamic_slice x17 -> x1, local copies, waits for them, and re-layouts: 8.88 us -> 0.08 us  [local(): lax.dynamic_slice(jnp.pad(cover, BAND), (view + BAND, view), (1, 2 * BAND...]
  transfers between devices with their start and end apart: 14 -> 26, of which waited for: 7 -> 10; matrix products, arithmetic and copies ran while one was open for 8% -> 0% of each run, Pallas kernels for 0% -> 0%
where the time goes in v1:
time: 186 us; the launch traced here: 185 us
  starting transfers between devices  68.8 us (37%)
  waiting for transfers between devices  62.3 us (33%)
  Pallas kernels  28.7 us (15%)
  between operations  14.4 us (8%)
  local copies, waits for them, and re-layouts  10.9 us (6%)
    ppermute x24, starting transfers between devices, passed(): lax.ppermute(value, ('seq', 'rep'), [(i, i + steps) for i in range(leadin...  68.8 us
    pallas_call x5, Pallas kernels, call(): pl.pallas_call(body, out_shape=[jax.ShapeDtypeStruct(s, d) for s, d in ou...  28.7 us
    all_gather x1, waiting for transfers between devices, local(): ups = lax.all_gather(up, ('seq', 'rep'))  25 us
    ppermute x24, waiting for transfers between devices, passed(): lax.ppermute(value, ('seq', 'rep'), [(i, i + steps) for i in range(leadin...  25 us
    all_gather x1, waiting for transfers between devices, local(): gathered = lax.all_gather(state, ('seq', 'rep'))  12.2 us
    unnamed x39, local copies, waits for them, and re-layouts  10.5 us
  transfers between devices with their start and end apart: 26, of which 10 were waited for; matrix products, arithmetic and copies ran while one was open for 0% of the time, Pallas kernels for 0%

profile of v1, /device:TPU:0, one launch (start us, length us, event | category | flops | bytes accessed | tf_op | source)
XLA Modules:
  0.0 185.1 jit_solution(13132127657475250111)
XLA Ops:
  11.3 2.1 %shard_map.120 = (bf16[2048,256]{1,0:T(8,128)(2,1)S(1)}, f32[256,512]{1,0:T(8,128)S(1)}, f32[256,512]{1,0:T(8,128)S(1)}, f32[256,512]{1,0:T(8,128)S(1)}, bf16[144,512]{1,0:T(8,128)(2,1)}) custom-call(bf16[256,512]{1,0:T(8,128)(2,1)S(1)} %copy-done.14, bf16[256,128]{1,0:T(8,128)(2,1)S(1)} %copy-done.6, bf16[256,128]{1,0:T(8,128)(2,1)S(1)} %copy-done.3, ...), custom_call_target="tpu_custom_call" | custom-call | tf_op jit(solution)/shard_map/pallas_call | solution.py:206
  13.5 1.3 collective-permute-start.4
  14.8 1.3 collective-permute-start.3
  16.1 3.7 %collective-permute-start.2 = (bf16[256,512]{1,0:T(8,128)(2,1)}, bf16[256,512]{1,0:T(8,128)(2,1)}, u32[]{:S(2)}, u32[]{:S(2)}) collective-permute-start(bf16[256,512]{1,0:T(8,128)(2,1)} %refs_6_.1), channel_id=1, source_target_pairs={{0,1},{1,4},{4,5},{5,8},{8,9},{9,12},{12,13},{2,3},{3,6},{6,7},{7,... | collective-permute-start | bytes 786440 | tf_op jit(solution)/shard_map/ppermute | solution.py:219
  19.9 5.6 %collective-permute-start.1 = (bf16[256,512]{1,0:T(8,128)(2,1)}, bf16[256,512]{1,0:T(8,128)(2,1)}, u32[]{:S(2)}, u32[]{:S(2)}) collective-permute-start(bf16[256,512]{1,0:T(8,128)(2,1)} %refs_6_.1), channel_id=1, source_target_pairs={{0,4},{1,5},{4,8},{5,9},{8,12},{9,13},{2,6},{3,7},{6,10},{7,11},{1... | collective-permute-start | bytes 786440 | tf_op jit(solution)/shard_map/ppermute | solution.py:219
  25.4 5.2 %collective-permute-start = (bf16[256,512]{1,0:T(8,128)(2,1)}, bf16[256,512]{1,0:T(8,128)(2,1)}, u32[]{:S(2)}, u32[]{:S(2)}) collective-permute-start(bf16[256,512]{1,0:T(8,128)(2,1)} %refs_6_.1), channel_id=1, source_target_pairs={{0,5},{1,8},{4,9},{5,12},{8,13},{2,7},{3,10},{6,11},{7,14},{10,15}... | collective-permute-start | bytes 786440 | tf_op jit(solution)/shard_map/ppermute | solution.py:219
  30.6 12.2 %all-gather.5.cloned.1.call-done = bf16[1152,512]{1,0:T(8,128)(2,1)} async-done(((bf16[144,512]{1,0:T(8,128)(2,1)}), bf16[1152,512]{1,0:T(8,128)(2,1)}) %all-gather.5.cloned.1.call-update) | async-done | bytes 1179664 | tf_op jit(solution)/shard_map/all_gather | solution.py:235
  47.2 1.3 collective-permute-start.11
  48.5 1.3 collective-permute-start.10
  49.8 1.3 collective-permute-start.9
  51.1 3.8 %collective-permute-start.8 = (bf16[256,512]{1,0:T(8,128)(2,1)S(1)}, bf16[256,512]{1,0:T(8,128)(2,1)}, u32[]{:S(2)}, u32[]{:S(2)}) collective-permute-start(bf16[256,512]{1,0:T(8,128)(2,1)S(1)} %shard_map.121.refs_13_), channel_id=1, source_target_pairs={{0,1},{1,4},{4,5},{5,8},{8,9},{9,12},{12,13},{2,3},{3,6},{6,7},{7,... | collective-permute-start | bytes 786440 | tf_op jit(solution)/shard_map/ppermute | solution.py:219
  54.9 4.1 %collective-permute-done.5.refs_9_ = bf16[256,512]{1,0:T(8,128)(2,1)S(1)} collective-permute-done((bf16[256,512]{1,0:T(8,128)(2,1)S(1)}, bf16[256,512]{1,0:T(8,128)(2,1)S(1)}, u32[]{:S(2)}, u32[]{:S(2)}) %collective-permute-start.5) | collective-permute-done | bytes 262176 | tf_op jit(solution)/shard_map/ppermute | solution.py:219
  59.0 8.1 %collective-permute-start.7 = (bf16[256,512]{1,0:T(8,128)(2,1)S(1)}, bf16[256,512]{1,0:T(8,128)(2,1)}, u32[]{:S(2)}, u32[]{:S(2)}) collective-permute-start(bf16[256,512]{1,0:T(8,128)(2,1)S(1)} %shard_map.121.refs_13_), channel_id=1, source_target_pairs={{0,4},{1,5},{4,8},{5,9},{8,12},{9,13},{2,6},{3,7},{6,10},{7,11},{1... | collective-permute-start | bytes 786440 | tf_op jit(solution)/shard_map/ppermute | solution.py:219
  67.1 2.2 %collective-permute-start.6 = (bf16[256,512]{1,0:T(8,128)(2,1)S(1)}, bf16[256,512]{1,0:T(8,128)(2,1)}, u32[]{:S(2)}, u32[]{:S(2)}) collective-permute-start(bf16[256,512]{1,0:T(8,128)(2,1)S(1)} %shard_map.121.refs_13_), channel_id=1, source_target_pairs={{0,5},{1,8},{4,9},{5,12},{8,13},{2,7},{3,10},{6,11},{7,14},{10,15}... | collective-permute-start | bytes 786440 | tf_op jit(solution)/shard_map/ppermute | solution.py:219
  70.2 4.4 %collective-permute-done.6.refs_10_ = bf16[256,512]{1,0:T(8,128)(2,1)} collective-permute-done((bf16[256,512]{1,0:T(8,128)(2,1)S(1)}, bf16[256,512]{1,0:T(8,128)(2,1)}, u32[]{:S(2)}, u32[]{:S(2)}) %collective-permute-start.6) | collective-permute-done | bytes 262176 | tf_op jit(solution)/shard_map/ppermute | solution.py:219
  75.6 23.1 %shard_map.122 = (bf16[256,512]{1,0:T(8,128)(2,1)}, bf16[256,512]{1,0:T(8,128)(2,1)}, bf16[7,256,512]{2,1,0:T(8,128)(2,1)S(1)}, bf16[7,256,512]{2,1,0:T(8,128)(2,1)}) custom-call(s32[1,7]{1,0:T(1,128)S(1)} %pad_dynamic-slice_fusion.refs_0_, bf16[256,512]{1,0:T(8,128)(2,1)S(1)} %copy-done.8, bf16[256,512]{1,0:T(8,128)(2,1)S(1)} %copy-done.9, ...), custom_call_target="tpu_custom_call" | custom-call | tf_op jit(solution)/shard_map/pallas_call | solution.py:206
  98.9 6.2 %collective-permute-start.22 = (bf16[256,512]{1,0:T(8,128)(2,1)S(1)}, bf16[256,512]{1,0:T(8,128)(2,1)S(1)}, u32[]{:S(2)}, u32[]{:S(2)}) collective-permute-start(bf16[256,512]{1,0:T(8,128)(2,1)S(1)} %get-tuple-element.35), channel_id=1, source_target_pairs={{0,5},{1,8},{4,9},{5,12},{8,13},{2,7},{3,10},{6,11},{7,14},{10,15}... | collective-permute-start | bytes 786440 | tf_op jit(solution)/shard_map/ppermute | solution.py:219
  105.1 4.9 %collective-permute-start.20 = (bf16[256,512]{1,0:T(8,128)(2,1)S(1)}, bf16[256,512]{1,0:T(8,128)(2,1)S(1)}, u32[]{:S(2)}, u32[]{:S(2)}) collective-permute-start(bf16[256,512]{1,0:T(8,128)(2,1)S(1)} %get-tuple-element.36), channel_id=1, source_target_pairs={{0,4},{1,5},{4,8},{5,9},{8,12},{9,13},{2,6},{3,7},{6,10},{7,11},{1... | collective-permute-start | bytes 786440 | tf_op jit(solution)/shard_map/ppermute | solution.py:219
  109.9 1.3 collective-permute-start.18
  111.2 1.3 collective-permute-start.16
  112.5 1.3 collective-permute-start.14
  114.0 1.3 collective-permute-start.12
  115.3 1.9 %collective-permute-done.20.refs_10_ = bf16[256,512]{1,0:T(8,128)(2,1)S(1)} collective-permute-done((bf16[256,512]{1,0:T(8,128)(2,1)S(1)}, bf16[256,512]{1,0:T(8,128)(2,1)S(1)}, u32[]{:S(2)}, u32[]{:S(2)}) %collective-permute-start.20) | collective-permute-done | bytes 262176 | tf_op jit(solution)/shard_map/ppermute | solution.py:219
  117.2 5.5 %collective-permute-start.23 = (bf16[256,512]{1,0:T(8,128)(2,1)S(1)}, bf16[256,512]{1,0:T(8,128)(2,1)S(1)}, u32[]{:S(2)}, u32[]{:S(2)}) collective-permute-start(bf16[256,512]{1,0:T(8,128)(2,1)S(1)} %get-tuple-element.28), channel_id=1, source_target_pairs={{0,5},{1,8},{4,9},{5,12},{8,13},{2,7},{3,10},{6,11},{7,14},{10,15}... | collective-permute-start | bytes 786440 | tf_op jit(solution)/shard_map/ppermute | solution.py:219
  122.7 4.4 %collective-permute-start.21 = (bf16[256,512]{1,0:T(8,128)(2,1)S(1)}, bf16[256,512]{1,0:T(8,128)(2,1)S(1)}, u32[]{:S(2)}, u32[]{:S(2)}) collective-permute-start(bf16[256,512]{1,0:T(8,128)(2,1)S(1)} %get-tuple-element.29), channel_id=1, source_target_pairs={{0,4},{1,5},{4,8},{5,9},{8,12},{9,13},{2,6},{3,7},{6,10},{7,11},{1... | collective-permute-start | bytes 786440 | tf_op jit(solution)/shard_map/ppermute | solution.py:219
  127.1 2.5 %collective-permute-start.19 = (bf16[256,512]{1,0:T(8,128)(2,1)S(1)}, bf16[256,512]{1,0:T(8,128)(2,1)S(1)}, u32[]{:S(2)}, u32[]{:S(2)}) collective-permute-start(bf16[256,512]{1,0:T(8,128)(2,1)S(1)} %get-tuple-element.30), channel_id=1, source_target_pairs={{0,1},{1,4},{4,5},{5,8},{8,9},{9,12},{12,13},{2,3},{3,6},{6,7},{7,... | collective-permute-start | bytes 786440 | tf_op jit(solution)/shard_map/ppermute | solution.py:219
  132.3 1.3 collective-permute-start.13
  134.0 11.9 %collective-permute-done.15.refs_3_ = bf16[256,512]{1,0:T(8,128)(2,1)S(1)} collective-permute-done((bf16[256,512]{1,0:T(8,128)(2,1)S(1)}, bf16[256,512]{1,0:T(8,128)(2,1)S(1)}, u32[]{:S(2)}, u32[]{:S(2)}) %collective-permute-start.15) | collective-permute-done | bytes 262176 | tf_op jit(solution)/shard_map/ppermute | solution.py:219
  145.9 1.4 collective-permute-done.13.refs_1_
  147.3 1.5 shard_map.123
  149.5 25.0 %all-gather.7.cloned.1.call-done = bf16[1024,512]{1,0:T(8,128)(2,1)} async-done(((bf16[128,512]{1,0:T(8,128)(2,1)}), bf16[1024,512]{1,0:T(8,128)(2,1)}) %all-gather.7.cloned.1.call-update) | async-done | bytes 1048592 | tf_op jit(solution)/shard_map/all_gather | solution.py:261
  176.7 1.5 shard_map.124
  (69 shorter events, 16.6 us)
Async XLA Ops:
  7.2 62.1 %copy-start.18 = (s32[8,8]{1,0:T(8,128)S(1)}, s32[8,8]{1,0:T(8,128)}, u32[]{:S(2)}) copy-start(s32[8,8]{1,0:T(8,128)} %param.16) | copy-start | bytes 772
  7.2 35.7 %all-gather.5.cloned.1.call-start = ((), (), s32[]{:S(2)}) async-start(), calls=%async_computation | async-start | bytes 1327104 | tf_op jit(solution)/shard_map/all_gather | solution.py:235
  11.3 63.3 %copy-start.8 = (bf16[256,512]{1,0:T(8,128)(2,1)S(1)}, bf16[256,512]{1,0:T(8,128)(2,1)}, u32[]{:S(2)}) copy-start(bf16[256,512]{1,0:T(8,128)(2,1)} %refs_1_.1) | copy-start | bytes 786436
  11.3 63.3 %copy-start.9 = (bf16[256,512]{1,0:T(8,128)(2,1)S(1)}, bf16[256,512]{1,0:T(8,128)(2,1)}, u32[]{:S(2)}) copy-start(bf16[256,512]{1,0:T(8,128)(2,1)} %refs_2_.1) | copy-start | bytes 786436
  13.5 161.1 %all-gather.7.cloned.1.call-start = ((), (), s32[]{:S(2)}) async-start(), calls=%async_computation.1 | async-start | bytes 1179648 | tf_op jit(solution)/shard_map/all_gather | solution.py:261
  13.5 31.9 %collective-permute-start.4 = (bf16[256,512]{1,0:T(8,128)(2,1)}, bf16[256,512]{1,0:T(8,128)(2,1)}, u32[]{:S(2)}, u32[]{:S(2)}) collective-permute-start(bf16[256,512]{1,0:T(8,128)(2,1)} %refs_6_.1), channel_id=1, source_target_pairs={{4,0},{5,1},{8,4},{9,5},{12,8},{13,9},{6,2},{7,3},{10,6},{11,7},{1... | collective-permute-start | bytes 786440 | tf_op jit(solution)/shard_map/ppermute | solution.py:219
  14.8 32.3 %collective-permute-start.3 = (bf16[256,512]{1,0:T(8,128)(2,1)}, bf16[256,512]{1,0:T(8,128)(2,1)}, u32[]{:S(2)}, u32[]{:S(2)}) collective-permute-start(bf16[256,512]{1,0:T(8,128)(2,1)} %refs_6_.1), channel_id=1, source_target_pairs={{1,0},{4,1},{5,4},{8,5},{9,8},{12,9},{13,12},{3,2},{6,3},{7,6},{10... | collective-permute-start | bytes 786440 | tf_op jit(solution)/shard_map/ppermute | solution.py:219
  16.1 32.4 %collective-permute-start.2 = (bf16[256,512]{1,0:T(8,128)(2,1)}, bf16[256,512]{1,0:T(8,128)(2,1)}, u32[]{:S(2)}, u32[]{:S(2)}) collective-permute-start(bf16[256,512]{1,0:T(8,128)(2,1)} %refs_6_.1), channel_id=1, source_target_pairs={{0,1},{1,4},{4,5},{5,8},{8,9},{9,12},{12,13},{2,3},{3,6},{6,7},{7,... | collective-permute-start | bytes 786440 | tf_op jit(solution)/shard_map/ppermute | solution.py:219
  19.9 29.9 %collective-permute-start.1 = (bf16[256,512]{1,0:T(8,128)(2,1)}, bf16[256,512]{1,0:T(8,128)(2,1)}, u32[]{:S(2)}, u32[]{:S(2)}) collective-permute-start(bf16[256,512]{1,0:T(8,128)(2,1)} %refs_6_.1), channel_id=1, source_target_pairs={{0,4},{1,5},{4,8},{5,9},{8,12},{9,13},{2,6},{3,7},{6,10},{7,11},{1... | collective-permute-start | bytes 786440 | tf_op jit(solution)/shard_map/ppermute | solution.py:219
  25.4 25.7 %collective-permute-start = (bf16[256,512]{1,0:T(8,128)(2,1)}, bf16[256,512]{1,0:T(8,128)(2,1)}, u32[]{:S(2)}, u32[]{:S(2)}) collective-permute-start(bf16[256,512]{1,0:T(8,128)(2,1)} %refs_6_.1), channel_id=1, source_target_pairs={{0,5},{1,8},{4,9},{5,12},{8,13},{2,7},{3,10},{6,11},{7,14},{10,15}... | collective-permute-start | bytes 786440 | tf_op jit(solution)/shard_map/ppermute | solution.py:219
  45.9 13.1 %collective-permute-start.5 = (bf16[256,512]{1,0:T(8,128)(2,1)S(1)}, bf16[256,512]{1,0:T(8,128)(2,1)S(1)}, u32[]{:S(2)}, u32[]{:S(2)}) collective-permute-start(bf16[256,512]{1,0:T(8,128)(2,1)S(1)} %copy-done.10), channel_id=1, source_target_pairs={{5,0},{8,1},{9,4},{12,5},{13,8},{7,2},{10,3},{11,6},{14,7},{15,10}... | collective-permute-start | bytes 786440 | tf_op jit(solution)/shard_map/ppermute | solution.py:219
  47.2 19.9 %collective-permute-start.11 = (bf16[256,512]{1,0:T(8,128)(2,1)S(1)}, bf16[256,512]{1,0:T(8,128)(2,1)S(1)}, u32[]{:S(2)}, u32[]{:S(2)}) collective-permute-start(bf16[256,512]{1,0:T(8,128)(2,1)S(1)} %shard_map.121.refs_13_), channel_id=1, source_target_pairs={{5,0},{8,1},{9,4},{12,5},{13,8},{7,2},{10,3},{11,6},{14,7},{15,10}... | collective-permute-start | bytes 786440 | tf_op jit(solution)/shard_map/ppermute | solution.py:219
  48.5 20.8 %collective-permute-start.10 = (bf16[256,512]{1,0:T(8,128)(2,1)S(1)}, bf16[256,512]{1,0:T(8,128)(2,1)}, u32[]{:S(2)}, u32[]{:S(2)}) collective-permute-start(bf16[256,512]{1,0:T(8,128)(2,1)S(1)} %shard_map.121.refs_13_), channel_id=1, source_target_pairs={{4,0},{5,1},{8,4},{9,5},{12,8},{13,9},{6,2},{7,3},{10,6},{11,7},{1... | collective-permute-start | bytes 786440 | tf_op jit(solution)/shard_map/ppermute | solution.py:219
  49.8 19.5 %collective-permute-start.9 = (bf16[256,512]{1,0:T(8,128)(2,1)S(1)}, bf16[256,512]{1,0:T(8,128)(2,1)}, u32[]{:S(2)}, u32[]{:S(2)}) collective-permute-start(bf16[256,512]{1,0:T(8,128)(2,1)S(1)} %shard_map.121.refs_13_), channel_id=1, source_target_pairs={{1,0},{4,1},{5,4},{8,5},{9,8},{12,9},{13,12},{3,2},{6,3},{7,6},{10... | collective-permute-start | bytes 786440 | tf_op jit(solution)/shard_map/ppermute | solution.py:219
  51.1 18.2 %collective-permute-start.8 = (bf16[256,512]{1,0:T(8,128)(2,1)S(1)}, bf16[256,512]{1,0:T(8,128)(2,1)}, u32[]{:S(2)}, u32[]{:S(2)}) collective-permute-start(bf16[256,512]{1,0:T(8,128)(2,1)S(1)} %shard_map.121.refs_13_), channel_id=1, source_target_pairs={{0,1},{1,4},{4,5},{5,8},{8,9},{9,12},{12,13},{2,3},{3,6},{6,7},{7,... | collective-permute-start | bytes 786440 | tf_op jit(solution)/shard_map/ppermute | solution.py:219
  59.0 11.3 %collective-permute-start.7 = (bf16[256,512]{1,0:T(8,128)(2,1)S(1)}, bf16[256,512]{1,0:T(8,128)(2,1)}, u32[]{:S(2)}, u32[]{:S(2)}) collective-permute-start(bf16[256,512]{1,0:T(8,128)(2,1)S(1)} %shard_map.121.refs_13_), channel_id=1, source_target_pairs={{0,4},{1,5},{4,8},{5,9},{8,12},{9,13},{2,6},{3,7},{6,10},{7,11},{1... | collective-permute-start | bytes 786440 | tf_op jit(solution)/shard_map/ppermute | solution.py:219
  67.1 7.5 %collective-permute-start.6 = (bf16[256,512]{1,0:T(8,128)(2,1)S(1)}, bf16[256,512]{1,0:T(8,128)(2,1)}, u32[]{:S(2)}, u32[]{:S(2)}) collective-permute-start(bf16[256,512]{1,0:T(8,128)(2,1)S(1)} %shard_map.121.refs_13_), channel_id=1, source_target_pairs={{0,5},{1,8},{4,9},{5,12},{8,13},{2,7},{3,10},{6,11},{7,14},{10,15}... | collective-permute-start | bytes 786440 | tf_op jit(solution)/shard_map/ppermute | solution.py:219
  98.9 15.2 %collective-permute-start.22 = (bf16[256,512]{1,0:T(8,128)(2,1)S(1)}, bf16[256,512]{1,0:T(8,128)(2,1)S(1)}, u32[]{:S(2)}, u32[]{:S(2)}) collective-permute-start(bf16[256,512]{1,0:T(8,128)(2,1)S(1)} %get-tuple-element.35), channel_id=1, source_target_pairs={{0,5},{1,8},{4,9},{5,12},{8,13},{2,7},{3,10},{6,11},{7,14},{10,15}... | collective-permute-start | bytes 786440 | tf_op jit(solution)/shard_map/ppermute | solution.py:219
  105.1 12.2 %collective-permute-start.20 = (bf16[256,512]{1,0:T(8,128)(2,1)S(1)}, bf16[256,512]{1,0:T(8,128)(2,1)S(1)}, u32[]{:S(2)}, u32[]{:S(2)}) collective-permute-start(bf16[256,512]{1,0:T(8,128)(2,1)S(1)} %get-tuple-element.36), channel_id=1, source_target_pairs={{0,4},{1,5},{4,8},{5,9},{8,12},{9,13},{2,6},{3,7},{6,10},{7,11},{1... | collective-permute-start | bytes 786440 | tf_op jit(solution)/shard_map/ppermute | solution.py:219
  109.9 12.8 %collective-permute-start.18 = (bf16[256,512]{1,0:T(8,128)(2,1)S(1)}, bf16[256,512]{1,0:T(8,128)(2,1)S(1)}, u32[]{:S(2)}, u32[]{:S(2)}) collective-permute-start(bf16[256,512]{1,0:T(8,128)(2,1)S(1)} %get-tuple-element.37), channel_id=1, source_target_pairs={{0,1},{1,4},{4,5},{5,8},{8,9},{9,12},{12,13},{2,3},{3,6},{6,7},{7,... | collective-permute-start | bytes 786440 | tf_op jit(solution)/shard_map/ppermute | solution.py:219
  111.2 15.9 %collective-permute-start.16 = (bf16[256,512]{1,0:T(8,128)(2,1)S(1)}, bf16[256,512]{1,0:T(8,128)(2,1)S(1)}, u32[]{:S(2)}, u32[]{:S(2)}) collective-permute-start(bf16[256,512]{1,0:T(8,128)(2,1)S(1)} %get-tuple-element.39), channel_id=1, source_target_pairs={{1,0},{4,1},{5,4},{8,5},{9,8},{12,9},{13,12},{3,2},{6,3},{7,6},{10... | collective-permute-start | bytes 786440 | tf_op jit(solution)/shard_map/ppermute | solution.py:219
  112.5 17.1 %collective-permute-start.14 = (bf16[256,512]{1,0:T(8,128)(2,1)S(1)}, bf16[256,512]{1,0:T(8,128)(2,1)S(1)}, u32[]{:S(2)}, u32[]{:S(2)}) collective-permute-start(bf16[256,512]{1,0:T(8,128)(2,1)S(1)} %get-tuple-element.40), channel_id=1, source_target_pairs={{4,0},{5,1},{8,4},{9,5},{12,8},{13,9},{6,2},{7,3},{10,6},{11,7},{1... | collective-permute-start | bytes 786440 | tf_op jit(solution)/shard_map/ppermute | solution.py:219
  113.9 33.5 %copy-start.5 = (bf16[256,128]{1,0:T(8,128)(2,1)S(1)}, bf16[256,128]{1,0:T(8,128)(2,1)}, u32[]{:S(2)}) copy-start(bf16[256,128]{1,0:T(8,128)(2,1)} %refs_14_.1) | copy-start | bytes 196612
  114.0 17.0 %collective-permute-start.12 = (bf16[256,512]{1,0:T(8,128)(2,1)S(1)}, bf16[256,512]{1,0:T(8,128)(2,1)S(1)}, u32[]{:S(2)}, u32[]{:S(2)}) collective-permute-start(bf16[256,512]{1,0:T(8,128)(2,1)S(1)} %get-tuple-element.41), channel_id=1, source_target_pairs={{5,0},{8,1},{9,4},{12,5},{13,8},{7,2},{10,3},{11,6},{14,7},{15,10}... | collective-permute-start | bytes 786440 | tf_op jit(solution)/shard_map/ppermute | solution.py:219
  117.2 15.1 %collective-permute-start.23 = (bf16[256,512]{1,0:T(8,128)(2,1)S(1)}, bf16[256,512]{1,0:T(8,128)(2,1)S(1)}, u32[]{:S(2)}, u32[]{:S(2)}) collective-permute-start(bf16[256,512]{1,0:T(8,128)(2,1)S(1)} %get-tuple-element.28), channel_id=1, source_target_pairs={{0,5},{1,8},{4,9},{5,12},{8,13},{2,7},{3,10},{6,11},{7,14},{10,15}... | collective-permute-start | bytes 786440 | tf_op jit(solution)/shard_map/ppermute | solution.py:219
  122.7 11.1 %collective-permute-start.21 = (bf16[256,512]{1,0:T(8,128)(2,1)S(1)}, bf16[256,512]{1,0:T(8,128)(2,1)S(1)}, u32[]{:S(2)}, u32[]{:S(2)}) collective-permute-start(bf16[256,512]{1,0:T(8,128)(2,1)S(1)} %get-tuple-element.29), channel_id=1, source_target_pairs={{0,4},{1,5},{4,8},{5,9},{8,12},{9,13},{2,6},{3,7},{6,10},{7,11},{1... | collective-permute-start | bytes 786440 | tf_op jit(solution)/shard_map/ppermute | solution.py:219
  127.1 6.7 %collective-permute-start.19 = (bf16[256,512]{1,0:T(8,128)(2,1)S(1)}, bf16[256,512]{1,0:T(8,128)(2,1)S(1)}, u32[]{:S(2)}, u32[]{:S(2)}) collective-permute-start(bf16[256,512]{1,0:T(8,128)(2,1)S(1)} %get-tuple-element.30), channel_id=1, source_target_pairs={{0,1},{1,4},{4,5},{5,8},{8,9},{9,12},{12,13},{2,3},{3,6},{6,7},{7,... | collective-permute-start | bytes 786440 | tf_op jit(solution)/shard_map/ppermute | solution.py:219
  129.7 4.3 %collective-permute-start.17 = (bf16[256,512]{1,0:T(8,128)(2,1)S(1)}, bf16[256,512]{1,0:T(8,128)(2,1)S(1)}, u32[]{:S(2)}, u32[]{:S(2)}) collective-permute-start(bf16[256,512]{1,0:T(8,128)(2,1)S(1)} %get-tuple-element.32), channel_id=1, source_target_pairs={{1,0},{4,1},{5,4},{8,5},{9,8},{12,9},{13,12},{3,2},{6,3},{7,6},{10... | collective-permute-start | bytes 786440 | tf_op jit(solution)/shard_map/ppermute | solution.py:219
  131.0 14.9 %collective-permute-start.15 = (bf16[256,512]{1,0:T(8,128)(2,1)S(1)}, bf16[256,512]{1,0:T(8,128)(2,1)S(1)}, u32[]{:S(2)}, u32[]{:S(2)}) collective-permute-start(bf16[256,512]{1,0:T(8,128)(2,1)S(1)} %get-tuple-element.33), channel_id=1, source_target_pairs={{4,0},{5,1},{8,4},{9,5},{12,8},{13,9},{6,2},{7,3},{10,6},{11,7},{1... | collective-permute-start | bytes 786440 | tf_op jit(solution)/shard_map/ppermute | solution.py:219
  132.3 15.0 %collective-permute-start.13 = (bf16[256,512]{1,0:T(8,128)(2,1)S(1)}, bf16[256,512]{1,0:T(8,128)(2,1)S(1)}, u32[]{:S(2)}, u32[]{:S(2)}) collective-permute-start(bf16[256,512]{1,0:T(8,128)(2,1)S(1)} %get-tuple-element.34), channel_id=1, source_target_pairs={{5,0},{8,1},{9,4},{12,5},{13,8},{7,2},{10,3},{11,6},{14,7},{15,10}... | collective-permute-start | bytes 786440 | tf_op jit(solution)/shard_map/ppermute | solution.py:219
  147.3 27.2 %copy-start.7 = (bf16[256,128]{1,0:T(8,128)(2,1)S(1)}, bf16[256,128]{1,0:T(8,128)(2,1)}, u32[]{:S(2)}) copy-start(bf16[256,128]{1,0:T(8,128)(2,1)} %b_ref.3) | copy-start | bytes 196612
  147.3 27.2 %copy-start.16 = (f32[8]{0:T(128)S(1)}, f32[8]{0:T(128)}, u32[]{:S(2)}) copy-start(f32[8]{0:T(128)} %param.13) | copy-start | bytes 100
  (13 other events, 52.6 us)
Sparse Core Ops, SparseCore 0:
  13.6 29.1 all-gather.4
  149.6 24.8 all-gather.6

commit v2 on v1

v2 whole, which is shorter than its diff:
```python
import functools

import jax
import jax.numpy as jnp
from jax import lax
from jax.experimental import pallas as pl
from jax.experimental.pallas import tpu as pltpu
from jax.sharding import PartitionSpec as P

HD = 64
BAND = 3
PAIR = 2 * HD
F32 = jnp.float32
BF16 = jnp.bfloat16
HIGHEST = lax.Precision.HIGHEST
SPAN = 2 * BAND + 1


def dot(a, b, dims):
    return lax.dot_general(a, b, (dims, ((), ())), preferred_element_type=F32)


NN = ((1,), (0,))
NT = ((1,), (1,))
TN = ((0,), (0,))


def first_lanes(shape):
    return lax.broadcasted_iota(jnp.int32, shape, 1) < HD


def widened(col, p):
    rows = col.shape[0]
    return jnp.where(
        first_lanes((rows, PAIR)),
        jnp.broadcast_to(col[:, 2 * p : 2 * p + 1], (rows, PAIR)),
        jnp.broadcast_to(col[:, 2 * p + 1 : 2 * p + 2], (rows, PAIR)),
    )


def widened_all(col):
    return jnp.concatenate([widened(col, p) for p in range(col.shape[1] // 2)], axis=1)


def stacked(a):
    first = first_lanes(a.shape)
    zero = jnp.zeros_like(a)
    return jnp.concatenate([jnp.where(first, a, zero), jnp.where(first, zero, a)], axis=0)


def picked(a):
    rows = a.shape[0] // 2
    return jnp.where(first_lanes((rows, PAIR)), a[:rows], a[rows:])


def running(keep):
    rows = keep.shape[0]
    below = (
        lax.broadcasted_iota(jnp.int32, (rows, rows), 0)
        >= lax.broadcasted_iota(jnp.int32, (rows, rows), 1)
    ).astype(F32)
    cumul = lax.dot_general(below, keep, (NN, ((), ())), precision=HIGHEST, preferred_element_type=F32)
    gain = jnp.sqrt(-one_less(2.0 * keep))
    return cumul, gain


def one_less(y):
    return jnp.tanh(0.5 * y) * (jnp.exp(y) + 1.0)


def step_decay(part, nstate):
    return part[nstate : nstate + 1, :].astype(F32) + part[nstate + 8 : nstate + 9, :].astype(F32)


def split_rows(total):
    total = jnp.broadcast_to(total, (8, total.shape[1]))
    high = total.astype(BF16)
    return jnp.concatenate([high, (total - high.astype(F32)).astype(BF16)], axis=0)


def whole(
    chips, x_ref, b_ref, c_ref, lk_ref, skip_ref, q_ref, k_ref, cover_ref, do_ref,
    att_ref, dq_ref, dk_ref, dx_ref,
    mix_ref, base_ref, ecum_ref, wide_ref, score_ref, inv_ref, k_buf, v_buf, g_out, g_in,
    own_ref, other_ref, tot_out, tot_in, acc_ref, edge_ref,
    k_send, k_recv, v_send, v_recv, g_send, g_recv, swap_send, swap_recv, tot_send, tot_recv, edge_send, edge_recv,
):
    z, r = lax.axis_index("seq"), lax.axis_index("rep")
    me = 2 * z + r
    views = 2 * chips
    rows, width = x_ref.shape
    nstate = b_ref.shape[1]
    heads = lk_ref.shape[1]
    pairs = width // PAIR
    half = width // 2
    offsets = [o for o in range(-BAND, BAND + 1) if o != 0]

    def there(o):
        return jnp.logical_and(me + o >= 0, me + o < views)

    def at_view(u):
        return {"seq": u // 2, "rep": u % 2}

    def remote(src, dst, send, recv, device):
        return pltpu.make_async_remote_copy(
            src_ref=src, dst_ref=dst, send_sem=send, recv_sem=recv,
            device_id=device, device_id_type=pl.DeviceIdType.MESH,
        )

    def key_copy(o):
        return remote(k_buf.at[BAND], k_buf.at[BAND - o], k_send.at[BAND + o], k_recv.at[BAND - o], at_view(me + o))

    def value_copy(o, p):
        return remote(
            v_buf.at[BAND, p], v_buf.at[BAND - o, p], v_send.at[BAND + o, p], v_recv.at[BAND - o, p], at_view(me + o)
        )

    def grad_copy(o, p):
        return remote(
            g_out.at[BAND + o, p], g_in.at[BAND - o, p], g_send.at[BAND + o, p], g_recv.at[BAND - o, p], at_view(me + o)
        )

    def key_came(o):
        remote(k_buf.at[BAND], k_buf.at[BAND + o], k_send.at[BAND + o], k_recv.at[BAND + o], at_view(me + o)).wait_recv()

    def value_came(o, p):
        remote(
            v_buf.at[BAND, p], v_buf.at[BAND + o, p], v_send.at[BAND + o, p], v_recv.at[BAND + o, p], at_view(me + o)
        ).wait_recv()

    def grad_came(o, p):
        remote(
            g_out.at[BAND + o, p], g_in.at[BAND + o, p], g_send.at[BAND + o, p], g_recv.at[BAND + o, p], at_view(me + o)
        ).wait_recv()

    core = {"seq": z, "rep": 1 - r}

    def swap(d):
        return remote(own_ref.at[d], other_ref.at[d], swap_send.at[d], swap_recv.at[d], core)

    def total_copy(d, to):
        return remote(
            tot_out.at[d], tot_in.at[d, z], tot_send.at[d, to], tot_recv.at[d, z], {"seq": to, "rep": r}
        )

    def total_came(d, source):
        remote(
            tot_out.at[d], tot_in.at[d, source], tot_send.at[d, source], tot_recv.at[d, source], {"seq": source, "rep": r}
        ).wait_recv()

    def edge_copy(d):
        return remote(edge_ref.at[d, r], edge_ref.at[d, r], edge_send.at[d], edge_recv.at[d], core)

    def edge_came(d):
        remote(edge_ref.at[d, r], edge_ref.at[d, 1 - r], edge_send.at[d], edge_recv.at[d], core).wait_recv()

    def onward(d, other):
        return other > z if d == 0 else other < z

    def behind(d, other):
        return other < z if d == 0 else other > z

    def put_state(d, state, total):
        for i in range(2):
            own_ref[d, i, 0:nstate, :] = state[:, i * half : (i + 1) * half].astype(BF16)
            own_ref[d, i, nstate : nstate + 16, :] = split_rows(total[:, i * half : (i + 1) * half])

    def send_totals(d):
        swap(d).wait_recv()
        mine, theirs = own_ref[d, r], other_ref[d, r]
        second = r == (1 if d == 0 else 0)
        mine_decay, their_decay = step_decay(mine, nstate), step_decay(theirs, nstate)
        mine, theirs = mine[:nstate].astype(F32), theirs[:nstate].astype(F32)
        factor = jnp.where(second, mine_decay, their_decay)
        total = jnp.where(second, factor * theirs + mine, factor * mine + theirs)
        tot_out[d, 0:nstate, :] = total.astype(BF16)
        tot_out[d, nstate : nstate + 16, :] = split_rows(mine_decay * their_decay)
        for to in range(chips):
            @pl.when(onward(d, to))
            def _(to=to):
                total_copy(d, to).start()

    def take_totals(d):
        acc_ref[...] = jnp.zeros_like(acc_ref)
        for source in range(chips) if d == 0 else range(chips - 1, -1, -1):
            @pl.when(behind(d, source))
            def _(source=source):
                total_came(d, source)
                part = tot_in[d, source]
                acc_ref[...] = step_decay(part, nstate) * acc_ref[...] + part[:nstate].astype(F32)
        edge_ref[d, r] = acc_ref[...].astype(BF16)
        edge_copy(d).start()
        edge_came(d)
        second = r == (1 if d == 0 else 0)
        sides = []
        for i in range(2):
            edge = edge_ref[d, i].astype(F32)
            part = other_ref[d, i]
            after = step_decay(part, nstate) * edge + part[:nstate].astype(F32)
            sides.append(jnp.where(second, after, edge).astype(BF16))
        return jnp.concatenate(sides, axis=1)

    barrier = pltpu.get_barrier_semaphore()
    for d in range(1, views):
        pl.semaphore_signal(
            barrier, inc=1, device_id=at_view((me + d) % views), device_id_type=pl.DeviceIdType.MESH
        )

    keep = lk_ref[...]
    cumul, gain = running(keep)
    last = cumul[rows - 1 : rows, :]
    total_decay = widened_all(jnp.exp(last))
    wide = widened_all(jnp.exp(last - cumul) * gain)
    wide_ref[...] = wide
    x = x_ref[...]
    put_state(0, dot(b_ref[...], (wide * x.astype(F32)).astype(BF16), TN), total_decay)
    for i in range(2):
        own_ref[1, i, nstate : nstate + 16, :] = own_ref[0, i, nstate : nstate + 16, :]
    for p in range(pairs):
        k_buf[BAND, p] = k_ref[:, p * PAIR : (p + 1) * PAIR]
    pl.semaphore_wait(barrier, views - 1)
    swap(0).start()
    for o in offsets:
        @pl.when(jnp.logical_not(there(o)))
        def _(o=o):
            k_buf[BAND + o] = jnp.zeros(k_buf.shape[1:], BF16)
            v_buf[BAND + o] = jnp.zeros(v_buf.shape[1:], BF16)

    ecum_ref[...] = widened_all(jnp.exp(cumul))
    send_totals(0)
    for o in (1, -1, 2, -2, 3, -3):
        @pl.when(there(o))
        def _(o=o):
            key_copy(o).start()

    both = jnp.transpose(jnp.concatenate([cumul, gain], axis=1))
    cross = dot(c_ref[...], b_ref[...], NT)
    lower = lax.broadcasted_iota(jnp.int32, (rows, rows), 0) >= lax.broadcasted_iota(
        jnp.int32, (rows, rows), 1
    )
    masked = jnp.where(lower, cross, 0.0)
    for p in range(pairs):
        mixes = []
        for h in (2 * p, 2 * p + 1):
            gaps = jnp.minimum(cumul[:, h : h + 1] - both[h : h + 1, :], 0.0)
            mix = (jnp.exp(gaps) * masked * both[heads + h : heads + h + 1, :]).astype(BF16)
            mix_ref[h * rows : (h + 1) * rows, :] = mix
            mixes.append(mix)
        xp = x_ref[:, p * PAIR : (p + 1) * PAIR]
        inner = dot(jnp.concatenate(mixes, axis=1), stacked(xp), NN)
        base_ref[:, p * PAIR : (p + 1) * PAIR] = inner + widened(skip_ref[...], p) * xp.astype(F32)

    entering = take_totals(0)
    c = c_ref[...]
    for p in range(pairs):
        lanes = slice(p * PAIR, (p + 1) * PAIR)
        carried = ecum_ref[:, lanes] * dot(c, entering[:, lanes], NN)
        v_buf[BAND, p] = (base_ref[:, lanes] + carried).astype(BF16)
        for o in (1, -1, 2, -2, 3, -3):
            @pl.when(there(o))
            def _(o=o, p=p):
                value_copy(o, p).start()

    biases = []
    for o in range(-BAND, BAND + 1):
        seen = cover_ref[me, jnp.clip(me + o, 0, views - 1)].astype(F32)
        biases.append((seen * there(o).astype(F32) - 1.0) * 1e30)
    order = [0, 1, -1, 2, -2, 3, -3]
    for o in offsets:
        @pl.when(there(o))
        def _(o=o):
            key_came(o)

    def scores(p, _):
        lanes = pl.ds(pl.multiple_of(p * PAIR, PAIR), PAIR)
        q2 = stacked(q_ref[:, lanes] * jnp.asarray(0.125, BF16))
        peak = None
        for j in range(SPAN):
            s = dot(q2, k_buf[j, p], NT) + biases[j]
            score_ref[p, j] = s
            peak = s if peak is None else jnp.maximum(peak, s)
        peak = jnp.max(peak, axis=1, keepdims=True)
        total = None
        for j in range(SPAN):
            e = jnp.exp(score_ref[p, j] - peak)
            score_ref[p, j] = e
            total = e if total is None else total + e
        inv = 1.0 / jnp.sum(total, axis=1, keepdims=True)
        inv_ref[p] = jnp.broadcast_to(inv, (2 * rows, PAIR))
        return 0

    lax.fori_loop(0, pairs, scores, 0)

    def attend(p, _):
        lanes = pl.ds(pl.multiple_of(p * PAIR, PAIR), PAIR)
        q2 = stacked(q_ref[:, lanes] * jnp.asarray(0.125, BF16))
        do2 = stacked(do_ref[:, lanes])
        inv = inv_ref[p][:, 0:1]
        for o in offsets:
            @pl.when(there(o))
            def _(o=o):
                value_came(o, p)
        out = jnp.zeros((2 * rows, PAIR), F32)
        for j in range(SPAN):
            share = score_ref[p, j] * inv
            score_ref[p, j] = share
            out += dot(share.astype(BF16), v_buf[j, p], NN)
        att = picked(out).astype(BF16)
        att_ref[:, lanes] = att
        att2 = jnp.concatenate([att, att], axis=0).astype(F32)
        corr = jnp.sum(do2.astype(F32) * att2, axis=1, keepdims=True)
        dq = jnp.zeros((2 * rows, PAIR), F32)
        for o in (3, -3, 2, -2, 1, -1, 0):
            j = BAND + o
            share = score_ref[p, j]
            dp = dot(do2, v_buf[j, p], NT)
            slope = (share * (dp - corr)).astype(BF16)
            dq += dot(slope, k_buf[j, p], NN)
            g_out[j, p, 0] = dot(slope, q2, TN).astype(BF16)
            g_out[j, p, 1] = dot(share.astype(BF16), do2, TN).astype(BF16)
            if o != 0:
                @pl.when(there(o))
                def _(o=o):
                    grad_copy(o, p).start()
        dq_ref[:, lanes] = (picked(dq) * 0.125).astype(BF16)
        return 0

    lax.fori_loop(0, pairs, attend, 0)

    ups = []
    for p in range(pairs):
        lanes = slice(p * PAIR, (p + 1) * PAIR)
        base_ref[:, 0:PAIR] = g_out[BAND, p, 0].astype(F32)
        base_ref[:, PAIR : 2 * PAIR] = g_out[BAND, p, 1].astype(F32)
        for o in (1, -1, 2, -2, 3, -3):
            @pl.when(there(o))
            def _(o=o, p=p):
                grad_came(o, p)
                base_ref[:, 0:PAIR] += g_in[BAND + o, p, 0].astype(F32)
                base_ref[:, PAIR : 2 * PAIR] += g_in[BAND + o, p, 1].astype(F32)
        dk_ref[:, lanes] = base_ref[:, 0:PAIR].astype(BF16)
        dv = base_ref[:, PAIR : 2 * PAIR].astype(BF16)
        dx_ref[:, lanes] = dv
        ups.append(dot(c, (ecum_ref[:, lanes] * dv.astype(F32)).astype(BF16), TN))
    up = jnp.concatenate(ups, axis=1)
    for i in range(2):
        own_ref[1, i, 0:nstate, :] = up[:, i * half : (i + 1) * half].astype(BF16)
    swap(1).start()
    send_totals(1)
    for p in range(pairs):
        lanes = slice(p * PAIR, (p + 1) * PAIR)
        dv = dx_ref[:, lanes]
        inner = dot(mix_ref[2 * p * rows : 2 * (p + 1) * rows, :], stacked(dv), TN)
        ecum_ref[:, lanes] = inner + widened(skip_ref[...], p) * dv.astype(F32)
    leaving = take_totals(1)
    carried = dot(b_ref[...], leaving, NN)
    dx_ref[...] = (ecum_ref[...] + wide_ref[...] * carried).astype(BF16)

    for o in offsets:
        @pl.when(there(o))
        def _(o=o):
            key_copy(o).wait_send()
            for p in range(pairs):
                value_copy(o, p).wait_send()
                grad_copy(o, p).wait_send()
    for d in range(2):
        swap(d).wait_send()
        edge_copy(d).wait_send()
        for to in range(chips):
            @pl.when(onward(d, to))
            def _(d=d, to=to):
                total_copy(d, to).wait_send()


def local(x, b, c, lk, skip, q, k, cover, do):
    rows, width = q.shape
    heads = lk.shape[1]
    nstate = b.shape[1]
    pairs = width // PAIR
    half = width // 2
    chips = lax.axis_size("seq")
    vmem = pl.BlockSpec(memory_space=pltpu.VMEM)
    smem = pl.BlockSpec(memory_space=pltpu.SMEM)
    dma = pltpu.SemaphoreType.DMA
    return pl.pallas_call(
        functools.partial(whole, chips),
        out_shape=[jax.ShapeDtypeStruct((rows, width), BF16)] * 4,
        in_specs=[vmem] * 7 + [smem, vmem],
        out_specs=[vmem] * 4,
        scratch_shapes=[
            pltpu.VMEM((heads * rows, rows), BF16),
            pltpu.VMEM((rows, width), F32),
            pltpu.VMEM((rows, width), F32),
            pltpu.VMEM((rows, width), F32),
            pltpu.VMEM((pairs, SPAN, 2 * rows, rows), F32),
            pltpu.VMEM((pairs, 2 * rows, PAIR), F32),
            pltpu.VMEM((SPAN, pairs, rows, PAIR), BF16),
            pltpu.VMEM((SPAN, pairs, rows, PAIR), BF16),
            pltpu.VMEM((SPAN, pairs, 2, rows, PAIR), BF16),
            pltpu.VMEM((SPAN, pairs, 2, rows, PAIR), BF16),
            pltpu.VMEM((2, 2, nstate + 16, half), BF16),
            pltpu.VMEM((2, 2, nstate + 16, half), BF16),
            pltpu.VMEM((2, nstate + 16, half), BF16),
            pltpu.VMEM((2, chips, nstate + 16, half), BF16),
            pltpu.VMEM((nstate, half), F32),
            pltpu.VMEM((2, 2, nstate, half), BF16),
            dma((SPAN,)), dma((SPAN,)),
            dma((SPAN, pairs)), dma((SPAN, pairs)),
            dma((SPAN, pairs)), dma((SPAN, pairs)),
            dma((2,)), dma((2,)),
            dma((2, chips)), dma((2, chips)),
            dma((2,)), dma((2,)),
        ],
        compiler_params=pltpu.CompilerParams(
            vmem_limit_bytes=56 << 20, collective_id=0, has_side_effects=True
        ),
    )(x, b, c, lk, skip.reshape(1, heads), q, k, cover, do)


def solution(mesh):
    rows = P(("groups", "seq", "rep"), "head")
    shared = P(("groups", "seq", "rep"), None)
    return jax.shard_map(
        local,
        mesh=mesh,
        in_specs=(rows, shared, shared, rows, P("head"), rows, rows, P("groups", None), rows),
        out_specs=(rows, rows, rows, rows),
        check_vma=False,
    )
```

time: 186 us -> 99.5 us (0.53)
  starting transfers between devices: 68.8 us -> 0 us
  Pallas kernels: 28.7 us -> 92.6 us
  waiting for transfers between devices: 62.3 us -> 0 us
  between operations: 14.4 us -> 0.65 us
  local copies, waits for them, and re-layouts: 10.9 us -> 5.99 us
    ppermute x24 -> x0, starting transfers between devices: 68.8 us -> none  [passed(): lax.ppermute(value, ('seq', 'rep'), [(i, i + steps) for i in range(leadin...]
    pallas_call x5 -> x1, Pallas kernels: 28.7 us -> 92.6 us  [local(): pl.pallas_call(functools.partial(whole, chips), out_shape=[jax.ShapeDtype...]
    all_gather x2 -> x0, waiting for transfers between devices: 37.2 us -> none  [the longest x1 25 us: local(): ups = lax.all_gather(up, ('seq', 'rep'))]
    ppermute x24 -> x0, waiting for transfers between devices: 25 us -> none  [passed(): lax.ppermute(value, ('seq', 'rep'), [(i, i + steps) for i in range(leadin...]
    unnamed x39 -> x11, local copies, waits for them, and re-layouts: 10.5 us -> 5.99 us
  transfers between devices with their start and end apart: 26 -> 0, of which waited for: 10 -> 0; matrix products, arithmetic and copies ran while one was open for 0% -> 0% of each run, Pallas kernels for 0% -> 0%
where the time goes in v2:
time: 99.5 us; the launch traced here: 99.3 us
  Pallas kernels  92.6 us (93%)
  local copies, waits for them, and re-layouts  5.99 us (6%)
    pallas_call x1, Pallas kernels, local(): pl.pallas_call(functools.partial(whole, chips), out_shape=[jax.ShapeDtype...  92.6 us
    unnamed x11, local copies, waits for them, and re-layouts  5.99 us

profile of v2, /device:TPU:0, one launch (start us, length us, event | category | flops | bytes accessed | tf_op | source)
XLA Modules:
  0.0 99.3 jit_solution(3992683267017292451)
XLA Ops:
  0.6 1.5 %copy.13.lk_ref = f32[256,8]{1,0:T(8,128)} copy(f32[256,8]{0,1:T(8,128)} %param.12) | data formatting | bytes 16384 | tf_op args[3]
  2.1 92.6 %shard_map.120 = (bf16[256,512]{1,0:T(8,128)(2,1)}, bf16[256,512]{1,0:T(8,128)(2,1)}, bf16[256,512]{1,0:T(8,128)(2,1)}, bf16[256,512]{1,0:T(8,128)(2,1)}) custom-call(bf16[256,512]{1,0:T(8,128)(2,1)} %x_ref.1, bf16[256,128]{1,0:T(8,128)(2,1)} %b_ref.1, bf16[256,128]{1,0:T(8,128)(2,1)} %c_ref.1, f32[256,8]{1,0:T(8,128)} %copy.13.lk_ref, f32[1,8]{1,0:T(1,128)} %bitcast.1, ...), custom_call_target="tpu_custom_call" | custom-call | tf_op jit(solution)/shard_map/pallas_call | solution.py:385
  94.8 0.0 copy-start.2
  94.8 1.7 %copy.18 = bf16[256,512]{1,0:T(8,128)(2,1)} copy(bf16[256,512]{1,0:T(8,128)(2,1)} %get-tuple-element.8) | data formatting | bytes 524288
  96.5 0.0 copy-done.2
  96.5 0.0 copy-start.1
  96.5 0.7 copy.19
  97.2 0.3 copy-done.1
  97.5 0.0 copy-start
  97.5 0.7 copy.20
  98.2 0.3 copy-done
  98.6 0.7 copy.21
Async XLA Ops:
  94.8 1.7 %copy-start.2 = (bf16[256,512]{1,0:T(8,128)(2,1)S(1)}, bf16[256,512]{1,0:T(8,128)(2,1)}, u32[]{:S(2)}) copy-start(bf16[256,512]{1,0:T(8,128)(2,1)} %get-tuple-element.9) | copy-start | bytes 786436
  96.5 1.0 %copy-start.1 = (bf16[256,512]{1,0:T(8,128)(2,1)S(1)}, bf16[256,512]{1,0:T(8,128)(2,1)}, u32[]{:S(2)}) copy-start(bf16[256,512]{1,0:T(8,128)(2,1)} %get-tuple-element.10) | copy-start | bytes 786436
  97.5 1.0 %copy-start = (bf16[256,512]{1,0:T(8,128)(2,1)S(1)}, bf16[256,512]{1,0:T(8,128)(2,1)}, u32[]{:S(2)}) copy-start(bf16[256,512]{1,0:T(8,128)(2,1)} %get-tuple-element.11) | copy-start | bytes 786436

commit v3 on v2

--- a/solution.py
+++ b/solution.py
@@ -83,7 +83,7 @@
     att_ref, dq_ref, dk_ref, dx_ref,
     mix_ref, base_ref, ecum_ref, wide_ref, score_ref, inv_ref, k_buf, v_buf, g_out, g_in,
     own_ref, other_ref, tot_out, tot_in, acc_ref, edge_ref,
-    k_send, k_recv, v_send, v_recv, g_send, g_recv, swap_send, swap_recv, tot_send, tot_recv, edge_send, edge_recv,
+    k_send, k_recv, v_send, v_recv, g_send, g_recv, swap_send, swap_recv, tot_send, tot_recv, edge_send, edge_recv, r_send,
 ):
     z, r = lax.axis_index("seq"), lax.axis_index("rep")
     me = 2 * z + r
@@ -134,6 +134,33 @@
         ).wait_recv()
 
     core = {"seq": z, "rep": 1 - r}
+    side = 1 - 2 * r
+
+    def direct(o):
+        if o in (2, -2):
+            return there(o)
+        if o in (1, -1):
+            return side == o
+        return jnp.logical_and(there(o), side * o < 0)
+
+    def key_relay(o):
+        return remote(
+            k_buf.at[BAND + o], k_buf.at[BAND + o - side], r_send.at[o // 2 + 1, pairs],
+            k_recv.at[BAND + o - side], core,
+        )
+
+    def value_relay(o, p):
+        return remote(
+            v_buf.at[BAND + o, p], v_buf.at[BAND + o - side, p], r_send.at[o // 2 + 1, p],
+            v_recv.at[BAND + o - side, p], core,
+        )
+
+    def relay_values(p):
+        for o in (2, -2):
+            @pl.when(there(o))
+            def _(o=o):
+                value_came(o, p)
+                value_relay(o, p).start()
 
     def swap(d):
         return remote(own_ref.at[d], other_ref.at[d], swap_send.at[d], swap_recv.at[d], core)
@@ -228,8 +255,8 @@
 
     ecum_ref[...] = widened_all(jnp.exp(cumul))
     send_totals(0)
-    for o in (1, -1, 2, -2, 3, -3):
-        @pl.when(there(o))
+    for o in (2, -2, 1, -1, 3, -3):
+        @pl.when(direct(o))
         def _(o=o):
             key_copy(o).start()
 
@@ -256,8 +283,8 @@
         lanes = slice(p * PAIR, (p + 1) * PAIR)
         carried = ecum_ref[:, lanes] * dot(c, entering[:, lanes], NN)
         v_buf[BAND, p] = (base_ref[:, lanes] + carried).astype(BF16)
-        for o in (1, -1, 2, -2, 3, -3):
-            @pl.when(there(o))
+        for o in (2, -2, 1, -1, 3, -3):
+            @pl.when(direct(o))
             def _(o=o, p=p):
                 value_copy(o, p).start()
 
@@ -266,7 +293,12 @@
         seen = cover_ref[me, jnp.clip(me + o, 0, views - 1)].astype(F32)
         biases.append((seen * there(o).astype(F32) - 1.0) * 1e30)
     order = [0, 1, -1, 2, -2, 3, -3]
-    for o in offsets:
+    for o in (2, -2):
+        @pl.when(there(o))
+        def _(o=o):
+            key_came(o)
+            key_relay(o).start()
+    for o in (1, -1, 3, -3):
         @pl.when(there(o))
         def _(o=o):
             key_came(o)
@@ -290,13 +322,14 @@
         return 0
 
     lax.fori_loop(0, pairs, scores, 0)
+    relay_values(0)
 
     def attend(p, _):
         lanes = pl.ds(pl.multiple_of(p * PAIR, PAIR), PAIR)
         q2 = stacked(q_ref[:, lanes] * jnp.asarray(0.125, BF16))
         do2 = stacked(do_ref[:, lanes])
         inv = inv_ref[p][:, 0:1]
-        for o in offsets:
+        for o in (1, -1, 3, -3):
             @pl.when(there(o))
             def _(o=o):
                 value_came(o, p)
@@ -307,6 +340,11 @@
             out += dot(share.astype(BF16), v_buf[j, p], NN)
         att = picked(out).astype(BF16)
         att_ref[:, lanes] = att
+
+        @pl.when(p < pairs - 1)
+        def _():
+            relay_values(p + 1)
+
         att2 = jnp.concatenate([att, att], axis=0).astype(F32)
         corr = jnp.sum(do2.astype(F32) * att2, axis=1, keepdims=True)
         dq = jnp.zeros((2 * rows, PAIR), F32)
@@ -359,10 +397,20 @@
     for o in offsets:
         @pl.when(there(o))
         def _(o=o):
+            for p in range(pairs):
+                grad_copy(o, p).wait_send()
+
+        @pl.when(direct(o))
+        def _(o=o):
             key_copy(o).wait_send()
             for p in range(pairs):
                 value_copy(o, p).wait_send()
-                grad_copy(o, p).wait_send()
+    for o in (2, -2):
+        @pl.when(there(o))
+        def _(o=o):
+            key_relay(o).wait_send()
+            for p in range(pairs):
+                value_relay(o, p).wait_send()
     for d in range(2):
         swap(d).wait_send()
         edge_copy(d).wait_send()
@@ -409,7 +457,7 @@
             dma((SPAN, pairs)), dma((SPAN, pairs)),
             dma((2,)), dma((2,)),
             dma((2, chips)), dma((2, chips)),
-            dma((2,)), dma((2,)),
+            dma((2,)), dma((2,)), dma((3, pairs + 1)),
         ],
         compiler_params=pltpu.CompilerParams(
             vmem_limit_bytes=56 << 20, collective_id=0, has_side_effects=True

time: 99.5 us -> 94.3 us (0.948)
  Pallas kernels: 92.6 us -> 87.2 us
    pallas_call x1, Pallas kernels: 92.6 us -> 87.2 us  [local(): pl.pallas_call(functools.partial(whole, chips), out_shape=[jax.ShapeDtype...]
where the time goes in v3:
time: 94.3 us; the launch traced here: 93.8 us
  Pallas kernels  87.2 us (92%)
  local copies, waits for them, and re-layouts  5.99 us (6%)
    pallas_call x1, Pallas kernels, local(): pl.pallas_call(functools.partial(whole, chips), out_shape=[jax.ShapeDtype...  87.2 us
    unnamed x11, local copies, waits for them, and re-layouts  5.99 us

profile of v3, /device:TPU:0, one launch (start us, length us, event | category | flops | bytes accessed | tf_op | source)
XLA Modules:
  0.0 93.8 jit_solution(11524732511451231791)
XLA Ops:
  0.6 1.5 %copy.13.lk_ref = f32[256,8]{1,0:T(8,128)} copy(f32[256,8]{0,1:T(8,128)} %param.12) | data formatting | bytes 16384 | tf_op args[3]
  2.1 87.2 %shard_map.120 = (bf16[256,512]{1,0:T(8,128)(2,1)}, bf16[256,512]{1,0:T(8,128)(2,1)}, bf16[256,512]{1,0:T(8,128)(2,1)}, bf16[256,512]{1,0:T(8,128)(2,1)}) custom-call(bf16[256,512]{1,0:T(8,128)(2,1)} %x_ref.1, bf16[256,128]{1,0:T(8,128)(2,1)} %b_ref.1, bf16[256,128]{1,0:T(8,128)(2,1)} %c_ref.1, f32[256,8]{1,0:T(8,128)} %copy.13.lk_ref, f32[1,8]{1,0:T(1,128)} %bitcast.1, ...), custom_call_target="tpu_custom_call" | custom-call | tf_op jit(solution)/shard_map/pallas_call | solution.py:433
  89.3 0.0 copy-start.2
  89.3 1.7 %copy.18 = bf16[256,512]{1,0:T(8,128)(2,1)} copy(bf16[256,512]{1,0:T(8,128)(2,1)} %get-tuple-element.8) | data formatting | bytes 524288
  91.0 0.0 copy-done.2
  91.0 0.0 copy-start.1
  91.0 0.7 copy.19
  91.7 0.3 copy-done.1
  92.1 0.0 copy-start
  92.1 0.7 copy.20
  92.8 0.3 copy-done
  93.1 0.7 copy.21
Async XLA Ops:
  89.3 1.7 %copy-start.2 = (bf16[256,512]{1,0:T(8,128)(2,1)S(1)}, bf16[256,512]{1,0:T(8,128)(2,1)}, u32[]{:S(2)}) copy-start(bf16[256,512]{1,0:T(8,128)(2,1)} %get-tuple-element.9) | copy-start | bytes 786436
  91.0 1.0 %copy-start.1 = (bf16[256,512]{1,0:T(8,128)(2,1)S(1)}, bf16[256,512]{1,0:T(8,128)(2,1)}, u32[]{:S(2)}) copy-start(bf16[256,512]{1,0:T(8,128)(2,1)} %get-tuple-element.10) | copy-start | bytes 786436
  92.1 1.0 %copy-start = (bf16[256,512]{1,0:T(8,128)(2,1)S(1)}, bf16[256,512]{1,0:T(8,128)(2,1)}, u32[]{:S(2)}) copy-start(bf16[256,512]{1,0:T(8,128)(2,1)} %get-tuple-element.11) | copy-start | bytes 786436

commit v4 on v3

--- a/solution.py
+++ b/solution.py
@@ -84,6 +84,7 @@
     mix_ref, base_ref, ecum_ref, wide_ref, score_ref, inv_ref, k_buf, v_buf, g_out, g_in,
     own_ref, other_ref, tot_out, tot_in, acc_ref, edge_ref,
     k_send, k_recv, v_send, v_recv, g_send, g_recv, swap_send, swap_recv, tot_send, tot_recv, edge_send, edge_recv, r_send,
+    x_in, x_send, x_recv,
 ):
     z, r = lax.axis_index("seq"), lax.axis_index("rep")
     me = 2 * z + r
@@ -154,6 +155,24 @@
             v_buf.at[BAND + o, p], v_buf.at[BAND + o - side, p], r_send.at[o // 2 + 1, p],
             v_recv.at[BAND + o - side, p], core,
         )
+
+    def indirect(o):
+        return jnp.logical_and(there(o), jnp.logical_not(direct(o)))
+
+    def term_copy(o, p):
+        i = int(o > 0)
+        return remote(g_out.at[BAND + o, p], x_in.at[i, p], x_send.at[i, p], x_recv.at[i, p], core)
+
+    def join_terms(p):
+        for o in (2, -2):
+            @pl.when(there(o))
+            def _(o=o):
+                term_copy(o, p).wait_recv()
+                for t in range(2):
+                    g_out[BAND + o, p, t] = (
+                        g_out[BAND + o, p, t].astype(F32) + x_in[int(o > 0), p, t].astype(F32)
+                    ).astype(BF16)
+                grad_copy(o, p).start()
 
     def relay_values(p):
         for o in (2, -2):
@@ -345,10 +364,14 @@
         def _():
             relay_values(p + 1)
 
+        @pl.when(p > 0)
+        def _():
+            join_terms(p - 1)
+
         att2 = jnp.concatenate([att, att], axis=0).astype(F32)
         corr = jnp.sum(do2.astype(F32) * att2, axis=1, keepdims=True)
         dq = jnp.zeros((2 * rows, PAIR), F32)
-        for o in (3, -3, 2, -2, 1, -1, 0):
+        for o in (3, -3, 1, -1, 2, -2, 0):
             j = BAND + o
             share = score_ref[p, j]
             dp = dot(do2, v_buf[j, p], NT)
@@ -356,22 +379,27 @@
             dq += dot(slope, k_buf[j, p], NN)
             g_out[j, p, 0] = dot(slope, q2, TN).astype(BF16)
             g_out[j, p, 1] = dot(share.astype(BF16), do2, TN).astype(BF16)
-            if o != 0:
-                @pl.when(there(o))
+            if o in (1, -1, 3, -3):
+                @pl.when(direct(o))
                 def _(o=o):
                     grad_copy(o, p).start()
+
+                @pl.when(indirect(o))
+                def _(o=o):
+                    term_copy(o, p).start()
         dq_ref[:, lanes] = (picked(dq) * 0.125).astype(BF16)
         return 0
 
     lax.fori_loop(0, pairs, attend, 0)
+    join_terms(pairs - 1)
 
     ups = []
     for p in range(pairs):
         lanes = slice(p * PAIR, (p + 1) * PAIR)
         base_ref[:, 0:PAIR] = g_out[BAND, p, 0].astype(F32)
         base_ref[:, PAIR : 2 * PAIR] = g_out[BAND, p, 1].astype(F32)
-        for o in (1, -1, 2, -2, 3, -3):
-            @pl.when(there(o))
+        for o in (1, -1, 3, -3, 2, -2):
+            @pl.when(direct(o))
             def _(o=o, p=p):
                 grad_came(o, p)
                 base_ref[:, 0:PAIR] += g_in[BAND + o, p, 0].astype(F32)
@@ -395,16 +423,17 @@
     dx_ref[...] = (ecum_ref[...] + wide_ref[...] * carried).astype(BF16)
 
     for o in offsets:
-        @pl.when(there(o))
-        def _(o=o):
-            for p in range(pairs):
-                grad_copy(o, p).wait_send()
-
         @pl.when(direct(o))
         def _(o=o):
             key_copy(o).wait_send()
             for p in range(pairs):
                 value_copy(o, p).wait_send()
+                grad_copy(o, p).wait_send()
+
+        @pl.when(indirect(o))
+        def _(o=o):
+            for p in range(pairs):
+                term_copy(o, p).wait_send()
     for o in (2, -2):
         @pl.when(there(o))
         def _(o=o):
@@ -458,6 +487,7 @@
             dma((2,)), dma((2,)),
             dma((2, chips)), dma((2, chips)),
             dma((2,)), dma((2,)), dma((3, pairs + 1)),
+            pltpu.VMEM((2, pairs, 2, rows, PAIR), BF16), dma((2, pairs)), dma((2, pairs)),
         ],
         compiler_params=pltpu.CompilerParams(
             vmem_limit_bytes=56 << 20, collective_id=0, has_side_effects=True

time: 94.3 us -> 82.6 us (0.88)
  Pallas kernels: 87.2 us -> 75.7 us
    pallas_call x1, Pallas kernels: 87.2 us -> 75.7 us  [local(): pl.pallas_call(functools.partial(whole, chips), out_shape=[jax.ShapeDtype...]
where the time goes in v4:
time: 82.6 us; the launch traced here: 82.3 us
  Pallas kernels  75.7 us (92%)
  local copies, waits for them, and re-layouts  5.99 us (7%)
    pallas_call x1, Pallas kernels, local(): pl.pallas_call(functools.partial(whole, chips), out_shape=[jax.ShapeDtype...  75.7 us
    unnamed x11, local copies, waits for them, and re-layouts  5.99 us

profile of v4, /device:TPU:0, one launch (start us, length us, event | category | flops | bytes accessed | tf_op | source)
XLA Modules:
  0.0 82.3 jit_solution(1571949981739028750)
XLA Ops:
  0.6 1.5 %copy.13.lk_ref = f32[256,8]{1,0:T(8,128)} copy(f32[256,8]{0,1:T(8,128)} %param.12) | data formatting | bytes 16384 | tf_op args[3]
  2.1 75.7 %shard_map.120 = (bf16[256,512]{1,0:T(8,128)(2,1)}, bf16[256,512]{1,0:T(8,128)(2,1)}, bf16[256,512]{1,0:T(8,128)(2,1)}, bf16[256,512]{1,0:T(8,128)(2,1)}) custom-call(bf16[256,512]{1,0:T(8,128)(2,1)} %x_ref.1, bf16[256,128]{1,0:T(8,128)(2,1)} %b_ref.1, bf16[256,128]{1,0:T(8,128)(2,1)} %c_ref.1, f32[256,8]{1,0:T(8,128)} %copy.13.lk_ref, f32[1,8]{1,0:T(1,128)} %bitcast.1, ...), custom_call_target="tpu_custom_call" | custom-call | tf_op jit(solution)/shard_map/pallas_call | solution.py:462
  77.8 0.0 copy-start.2
  77.8 1.7 %copy.18 = bf16[256,512]{1,0:T(8,128)(2,1)} copy(bf16[256,512]{1,0:T(8,128)(2,1)} %get-tuple-element.8) | data formatting | bytes 524288
  79.5 0.0 copy-done.2
  79.5 0.0 copy-start.1
  79.5 0.7 copy.19
  80.2 0.3 copy-done.1
  80.6 0.0 copy-start
  80.6 0.7 copy.20
  81.3 0.3 copy-done
  81.6 0.7 copy.21
Async XLA Ops:
  77.8 1.7 %copy-start.2 = (bf16[256,512]{1,0:T(8,128)(2,1)S(1)}, bf16[256,512]{1,0:T(8,128)(2,1)}, u32[]{:S(2)}) copy-start(bf16[256,512]{1,0:T(8,128)(2,1)} %get-tuple-element.9) | copy-start | bytes 786436
  79.5 1.0 %copy-start.1 = (bf16[256,512]{1,0:T(8,128)(2,1)S(1)}, bf16[256,512]{1,0:T(8,128)(2,1)}, u32[]{:S(2)}) copy-start(bf16[256,512]{1,0:T(8,128)(2,1)} %get-tuple-element.10) | copy-start | bytes 786436
  80.6 1.0 %copy-start = (bf16[256,512]{1,0:T(8,128)(2,1)S(1)}, bf16[256,512]{1,0:T(8,128)(2,1)}, u32[]{:S(2)}) copy-start(bf16[256,512]{1,0:T(8,128)(2,1)} %get-tuple-element.11) | copy-start | bytes 786436
